TPU v7x, 512 devices: a whole 4x8x8 slice. The times are simulated.
512 devices in a mesh: stack: 16 (over y, core), flow: 8 (over z), width: 4 (over x).
Axes of the slice: x: 4, y: 8, z: 8, core: 2. Of those that a mesh axis runs over, the one named last changes fastest.
Arguments:
- initial_thermal_state: float32 [256, 1024, 1024], P('stack', 'flow', 'width'), may hold values from -6 to 6
- plate_fluid_category: int32 [256], replicated, may hold values from 0 to 2
- corrugation_type_grid: int32 [256, 1024], P('stack', 'flow'), may hold values from 0 to 3
Outputs:
- new_temperature: float32 [256, 1024, 1024], P('stack', 'flow', 'width')
Inputs may be any that keep to these rules, and one draw needn't show every extreme that they name: `plate_fluid_category`: 0 is a hot stream layer, 1 a cold stream layer, 2 a parting sheet. `corrugation_type_grid`: selects a column of the conductivity and film tables.
All inputs are finite; a program needn't handle non-finite values.
Results may differ from a plain program's by a relative error of at most 0.0003.
Values sent between devices are 32-bit elements; how exact they have to be, the bound alone decides.
A program may use at most 64 MiB of HBM per device.

v0:
```python
import jax
import jax.numpy as jnp
from jax import lax
from jax.sharding import PartitionSpec as P

stack_conductance = (0.15, 0.25, 1.0)
plane_conductance = ((0.35, 0.5, 0.7, 0.9), (0.3, 0.45, 0.65, 0.85), (0.8, 0.9, 1.0, 0.95))
film_coefficient = ((0.4, 0.8, 1.2, 1.6), (0.3, 0.6, 1.0, 1.4), (0.0, 0.0, 0.0, 0.0))
stream_level = (1.5, -1.0, 0.0)
inplane_update = 0.24
stack_scale = 0.2


def with_halo(x, sides, width):
    for axis, dim in sides:
        devices, length = (lax.axis_size(axis), x.shape[dim])
        up = [(i, (i + 1) % devices) for i in range(devices - 1)]
        down = [(j, i) for i, j in up]
        last = lax.slice_in_dim(x, length - width, length, axis=dim)
        first = lax.slice_in_dim(x, 0, width, axis=dim)
        before = lax.ppermute(last, axis, up)
        after = lax.ppermute(first, axis, down)
        x = jnp.concatenate([before, x, after], axis=dim)
    return x


def from_behind(value, axis, steps):
    count = lax.axis_size(axis)
    first, last = (max(0, -steps), min(count, count - steps))
    return lax.ppermute(value, axis, [(source, source + steps) for source in range(first, last)])


def face_weight(centre, beside):
    return 2.0 * centre * beside / (centre + beside)


def inplane_flux(padded_t, padded_k, centre_t, centre_k):
    accumulated = face_weight(centre_k, padded_k[..., 2:, 1:-1]) * (
        padded_t[..., 2:, 1:-1] - centre_t
    )
    accumulated = accumulated + face_weight(centre_k, padded_k[..., :-2, 1:-1]) * (
        padded_t[..., :-2, 1:-1] - centre_t
    )
    accumulated = accumulated + face_weight(centre_k, padded_k[..., 1:-1, 2:]) * (
        padded_t[..., 1:-1, 2:] - centre_t
    )
    accumulated = accumulated + face_weight(centre_k, padded_k[..., 1:-1, :-2]) * (
        padded_t[..., 1:-1, :-2] - centre_t
    )
    return accumulated


def broaden(plane_part, template):
    return plane_part.reshape(plane_part.shape + (1,) * (template.ndim - plane_part.ndim))


def thomas_solve(below_link, diagonal, above_link, rhs_list):

    def forward(state_now, row_data):
        ratio_prev, partial_prev = state_now
        link_low, middle, link_high, rights = row_data
        pivot_value = middle - link_low * ratio_prev
        ratio_now = link_high / pivot_value
        partial_now = tuple(
            (
                (item + broaden(link_low, item) * prior) / broaden(pivot_value, item)
                for item, prior in zip(rights, partial_prev)
            )
        )
        return ((ratio_now, partial_now), (ratio_now, partial_now))

    start_state = (
        jnp.zeros_like(diagonal[0]),
        tuple((jnp.zeros_like(item[0]) for item in rhs_list)),
    )
    _, (ratios, partials) = lax.scan(
        forward, start_state, (below_link, diagonal, above_link, tuple(rhs_list))
    )

    def backward(following, row_data):
        ratio_now, partial_now = row_data
        values = tuple(
            (part + broaden(ratio_now, part) * later for part, later in zip(partial_now, following))
        )
        return (values, values)

    start_values = tuple((jnp.zeros_like(item[0]) for item in rhs_list))
    _, solved = lax.scan(backward, start_values, (ratios, partials), reverse=True)
    return solved


def select_one(code_array, table_values):
    width_count = len(table_values)
    onehot = (code_array[..., None] == jnp.arange(width_count, dtype=jnp.int32)).astype(jnp.float32)
    return jnp.sum(onehot * jnp.asarray(table_values, jnp.float32), -1)


def select_two(type_codes, fin_codes, table_values):
    type_onehot = (type_codes[:, None] == jnp.arange(3, dtype=jnp.int32)).astype(jnp.float32)
    table_rows = jnp.sum(type_onehot[:, :, None] * jnp.asarray(table_values, jnp.float32)[None], 1)
    fin_onehot = (fin_codes[..., None] == jnp.arange(4, dtype=jnp.int32)).astype(jnp.float32)
    return jnp.sum(fin_onehot * table_rows[:, None, :], -1)


def per_device(initial_thermal_state, plate_fluid_category, corrugation_type_grid):
    sheet_group_portion, streamwise_portion, spanwise_portion = initial_thermal_state.shape
    stack_count = lax.axis_size("stack")
    position = lax.axis_index("stack")
    layers_all = sheet_group_portion * stack_count
    stack_k = select_one(plate_fluid_category, stack_conductance)
    coupling = stack_scale * float(layers_all * layers_all) * face_weight(stack_k[:-1], stack_k[1:])
    upper_all = jnp.concatenate([coupling, jnp.zeros((1,), jnp.float32)])
    lower_all = jnp.concatenate([jnp.zeros((1,), jnp.float32), coupling])
    offset = position * sheet_group_portion
    upper_own = lax.dynamic_slice_in_dim(upper_all, offset, sheet_group_portion)
    lower_own = lax.dynamic_slice_in_dim(lower_all, offset, sheet_group_portion)
    types_own = lax.dynamic_slice_in_dim(plate_fluid_category, offset, sheet_group_portion)
    lateral_transmission = select_two(types_own, corrugation_type_grid, plane_conductance)
    surface_coefficient_map = select_two(types_own, corrugation_type_grid, film_coefficient)
    level_local_shard = select_one(types_own, stream_level)
    thermal_transmission_map = jnp.broadcast_to(
        lateral_transmission[:, :, None], initial_thermal_state.shape
    )
    bordered_grid = with_halo(
        jnp.stack([initial_thermal_state, thermal_transmission_map]), (("flow", 2), ("width", 3)), 1
    )
    stack_heat_flux = inplane_flux(
        bordered_grid[0], bordered_grid[1], initial_thermal_state, thermal_transmission_map
    )
    linear_system_target = (
        initial_thermal_state
        + inplane_update * stack_heat_flux
        + (surface_coefficient_map * level_local_shard[:, None])[:, :, None]
    )
    diagonal = 1.0 + surface_coefficient_map + lower_own[:, None] + upper_own[:, None]
    interior = sheet_group_portion - 1
    below_in = jnp.broadcast_to(lower_own[:interior, None], (interior, streamwise_portion))
    above_in = jnp.broadcast_to(upper_own[:interior, None], (interior, streamwise_portion))
    from_below = jnp.zeros((interior, streamwise_portion), jnp.float32).at[0].set(lower_own[0])
    from_above = (
        jnp.zeros((interior, streamwise_portion), jnp.float32)
        .at[interior - 1]
        .set(upper_own[interior - 1])
    )
    local_part, below_resp, above_resp = thomas_solve(
        below_in,
        diagonal[:interior],
        above_in,
        (linear_system_target[:interior], from_below, from_above),
    )
    next_first, next_below, next_above = from_behind(
        (local_part[0], below_resp[0], above_resp[0]), "stack", -1
    )
    edge_below = lower_own[interior]
    edge_above = upper_own[interior]
    red_below = edge_below * below_resp[interior - 1]
    red_diag = diagonal[interior] - edge_below * above_resp[interior - 1] - edge_above * next_below
    red_above = edge_above * next_above
    red_right = (
        linear_system_target[interior]
        + edge_below * local_part[interior - 1]
        + edge_above * next_first
    )
    all_below, all_diag, all_above, all_right = (
        lax.all_gather(red_below[None], "stack", axis=0, tiled=True),
        lax.all_gather(red_diag[None], "stack", axis=0, tiled=True),
        lax.all_gather(red_above[None], "stack", axis=0, tiled=True),
        lax.all_gather(red_right[None], "stack", axis=0, tiled=True),
    )
    solved = thomas_solve(all_below, all_diag, all_above, (all_right,))[0]
    own_value = lax.dynamic_index_in_dim(solved, position, 0, keepdims=False)
    prev_value = lax.dynamic_index_in_dim(solved, jnp.maximum(position - 1, 0), 0, keepdims=False)
    prev_value = prev_value * (position > 0).astype(jnp.float32)
    interior_values = (
        local_part
        + below_resp[:, :, None] * prev_value[None]
        + above_resp[:, :, None] * own_value[None]
    )
    return jnp.concatenate([interior_values, own_value[None]], 0)


def solution(mesh):
    placed = (P("stack", "flow", "width"), P(), P("stack", "flow"))
    return jax.shard_map(
        per_device,
        mesh=mesh,
        in_specs=placed,
        out_specs=P("stack", "flow", "width"),
        check_vma=False,
    )
```

profile of v0, /device:TPU:1, one launch (start us, length us, event | category | flops | bytes accessed | tf_op | source)
XLA Modules:
  0.0 226.5 jit_solution(10392655078989039629)
XLA Ops:
  9.5 4.8 %collective-permute-start = (f32[2,16,1,256]{3,1,2,0:T(8,128)S(1)}, f32[2,16,1,256]{3,1,2,0:T(8,128)S(1)}, u32[]{:S(2)}, u32[]{:S(2)}) collective-permute-start(f32[2,16,1,256]{3,1,2,0:T(8,128)S(1)} %copy.50), channel_id=1, source_target_pairs={{0,4},{4,8},{8,12},{12,16},{16,20},{20,24},{24,28},{1,5},{5,9},{9,... | collective-permute-start | bytes 98312 | tf_op jit(solution)/shard_map/ppermute | solution.py:21
  16.3 3.3 %collective-permute-done.1 = f32[2,16,1,256]{3,1,2,0:T(8,128)S(1)} collective-permute-done((f32[2,16,1,256]{3,1,2,0:T(8,128)S(1)}, f32[2,16,1,256]{3,1,2,0:T(8,128)S(1)}, u32[]{:S(2)}, u32[]{:S(2)}) %collective-permute-start.1) | collective-permute-done | bytes 32800 | tf_op jit(solution)/shard_map/ppermute | solution.py:22
  20.1 2.8 %fusion.53 = (f32[2,16,130,1]{3,2,1,0:T(8,128)}, f32[2,16,130,1]{3,2,1,0:T(8,128)}) fusion(f32[2,16,130,256]{3,2,1,0:T(8,128)S(1)} %pad_maximum_fusion.1), kind=kLoop, calls=%fused_computation.114 | loop fusion | bytes 66560 | tf_op jit(solution)/shard_map/slice | solution.py:19
  22.9 2.8 %copy.54 = f32[2,16,130,1]{2,1,3,0:T(8,128)S(1)} copy(f32[2,16,130,1]{3,2,1,0:T(8,128)} %get-tuple-element.778) | data formatting | bytes 33280 | tf_op jit(solution)/shard_map/slice | solution.py:19
  25.7 3.1 %collective-permute-start.2 = (f32[2,16,130,1]{2,1,3,0:T(8,128)S(1)}, f32[2,16,130,1]{2,1,3,0:T(8,128)S(1)}, u32[]{:S(2)}, u32[]{:S(2)}) collective-permute-start(f32[2,16,130,1]{2,1,3,0:T(8,128)S(1)} %copy.54), channel_id=1, source_target_pairs={{0,1},{1,2},{2,3},{4,5},{5,6},{6,7},{8,9},{9,10},{10,11},{12,13},{... | collective-permute-start | bytes 49928 | tf_op jit(solution)/shard_map/ppermute | solution.py:21
  28.8 2.8 %copy.55 = f32[2,16,130,1]{2,1,3,0:T(8,128)S(1)} copy(f32[2,16,130,1]{3,2,1,0:T(8,128)} %get-tuple-element.779) | data formatting | bytes 33280 | tf_op jit(solution)/shard_map/slice | solution.py:20
  34.3 2.1 copy.56
  36.4 2.1 copy.57
  38.6 6.4 %pad_maximum_fusion = f32[2,16,130,258]{3,2,1,0:T(8,128)S(1)} fusion(f32[2,16,130,1]{3,2,1,0:T(8,128)} %copy.57, f32[2,16,1,256]{3,2,1,0:T(1,128)S(1)} %copy.53, f32[1,16,128,256]{3,2,1,0:T(8,128)S(1)} %stack_broadcast_in_dim.2, f32[1,16,128,256]{3,2,1,0:T(8,128)} %bitcast.149, f32[2,16,1,256]{3,2,1,0:T(1,128)S(1)} %copy.52, f32[2,16,130,1]{3,2,1,0:T(8,128)} %copy.56), kind=kLoop, calls=%fused_computation.60 | loop fusion | flops 5366400 | bytes 8586240 | tf_op jit(solution)/shard_map/concatenate | solution.py:23
  46.6 4.7 %fusion.34 = f32[16,128,256]{2,1,0:T(8,128)S(1)} fusion(f32[16,128,256]{2,1,0:T(8,128)S(1)} %copy-done.1, f32[16,130,258]{2,1,0:T(8,128)S(1)} %get-tuple-element.777, f32[16,130,258]{2,1,0:T(8,128)S(1)} %get-tuple-element.776, f32[16,128]{1,0:T(8,128)S(1)} %get-tuple-element.786, f32[16,128]{1,0:T(8,128)S(1)} %get-tuple-element.675, ...), kind=kLoop, calls=%fused_computation.69 | loop fusion | flops 13631488 | bytes 20996096 | tf_op jit(solution)/shard_map/add | solution.py:131
  51.3 1.7 slice.167
  53.5 18.0 %while.86 = (s32[]{:T(128)}, f32[128]{0:T(128)S(1)}, f32[128,256]{1,0:T(8,128)S(1)}, f32[128]{0:T(128)S(1)}, f32[128]{0:T(128)S(1)}, /*index=5*/f32[15,128]{1,0:...) while((s32[]{:T(128)}, f32[128]{0:T(128)S(1)}, ...), condition=%wide.region_7.0_spmd.clone, body=%wide.region_6.0_spmd.clone.sunk | while | flops 132611 | bytes 536257 | solution.py:76
  73.0 17.2 %while.87 = (s32[]{:T(128)}, f32[128,256]{1,0:T(8,128)S(1)}, f32[128]{0:T(128)S(1)}, f32[128]{0:T(128)S(1)}, f32[15,128,256]{2,1,0:T(8,128)S(1)}, /*index=5*/f32...) while((s32[]{:T(128)}, f32[128,256]{1,0:T(8,128)S(1)}, ...), condition=%wide.region_9.10_spmd.clone, body=%wide.region_8.9_spmd.clone.sunk | while | flops 99076 | bytes 531633 | solution.py:88
  90.3 5.0 %collective-permute-start.6 = (f32[128,256]{1,0:T(8,128)S(1)}, f32[128,256]{1,0:T(8,128)S(1)}, u32[]{:S(2)}, u32[]{:S(2)}) collective-permute-start(f32[128,256]{1,0:T(8,128)S(1)} %slice_bitcast_fusion.2), channel_id=1, source_target_pairs={{32,0},{64,32},{96,64},{128,96},{160,128},{192,160},{224,192},{256... | collective-permute-start | bytes 393224 | tf_op jit(solution)/shard_map/ppermute | solution.py:30
  96.0 3.2 %collective-permute-done.6 = f32[128,256]{1,0:T(8,128)S(1)} collective-permute-done((f32[128,256]{1,0:T(8,128)S(1)}, f32[128,256]{1,0:T(8,128)S(1)}, u32[]{:S(2)}, u32[]{:S(2)}) %collective-permute-start.6) | collective-permute-done | bytes 131104 | tf_op jit(solution)/shard_map/ppermute | solution.py:30
  99.1 2.9 %fusion.41 = f32[128,256]{1,0:T(8,128)} fusion(f32[16,128,256]{2,1,0:T(8,128)} %copy-done.2, f32[128,256]{1,0:T(8,128)S(1)} %collective-permute-done.6, f32[15,128,256]{2,1,0:T(8,128)S(1)} %get-tuple-element.483, f32[]{:T(128)} %bitcast.3, f32[]{:T(128)} %bitcast.7), kind=kLoop, calls=%fused_computation.82 | loop fusion | flops 131072 | bytes 524296 | tf_op jit(solution)/shard_map/add | solution.py:160
  102.8 1.9 collective-permute-start.5
  104.8 18.0 %all-gather.5 = f32[16,1,128]{2,1,0:T(1,128)S(1)} all-gather(f32[1,1,128]{2,1,0:T(1,128)S(1)} %get-tuple-element.784), channel_id=1, replica_groups=mesh['stack'=16,'flow'=8,'width'=4] {'stack'}, dimensions={0}, use_global_device_ids=true | all-gather | bytes 8704 | tf_op jit(solution)/shard_map/all_gather | solution.py:165
  122.7 2.1 collective-permute-start.4
  126.2 16.0 %all-gather.4 = f32[16,1,128]{2,1,0:T(1,128)S(1)} all-gather(f32[1,1,128]{2,1,0:T(1,128)S(1)} %fusion.46), channel_id=3, replica_groups=mesh['stack'=16,'flow'=8,'width'=4] {'stack'}, dimensions={0}, use_global_device_ids=true | all-gather | bytes 8704 | tf_op jit(solution)/shard_map/all_gather | solution.py:166
  142.9 16.1 %all-gather.3 = f32[16,1,128]{2,1,0:T(1,128)S(1)} all-gather(f32[1,1,128]{2,1,0:T(1,128)S(1)} %multiply_bitcast_fusion.2), channel_id=2, replica_groups=mesh['stack'=16,'flow'=8,'width'=4] {'stack'}, dimensions={0}, use_global_device_ids=true | all-gather | bytes 8704 | tf_op jit(solution)/shard_map/all_gather | solution.py:167
  160.5 27.9 %while.88 = (s32[]{:T(128)}, f32[128]{0:T(128)S(1)}, f32[128,256]{1,0:T(8,128)S(1)}, f32[16,128]{1,0:T(8,128)S(1)}, f32[16,128,256]{2,1,0:T(8,128)}, /*index=5*/...) while((s32[]{:T(128)}, f32[128]{0:T(128)S(1)}, ...), condition=%wide.region_11.12_spmd.clone, body=%wide.region_10.11_spmd.clone.sunk | while | flops 131587 | bytes 531076 | solution.py:76
  172.7 1.7 bitcast_dynamic-update-slice_fusion.10
  189.9 26.6 %while.89 = (s32[]{:T(128)}, f32[128,256]{1,0:T(8,128)S(1)}, f32[16,128,256]{2,1,0:T(8,128)}, f32[16,128,256]{2,1,0:T(8,128)}, f32[16,128]{1,0:T(8,128)S(1)}, /*index=5*/s32[]{:T(128)}, s32[]{:T(128)}, s32[]{:T(128)}) while((s32[]{:T(128)}, f32[128,256]{1,0:T(8,128)S(1)}, f32[16,128,256]{2,1,0:T(8,128)}, ...), condition=%wide.region_13.14_spmd.clone, body=%wide.region_12.13_spmd.clone.sunk | while | flops 98308 | bytes 525939 | solution.py:88
  (341 shorter events, 108.0 us)
Async XLA Ops:
  6.5 152.4 %all-gather.8.cloned.1.call-start = ((), (), s32[]{:S(2)}) async-start(), calls=%async_computation | async-start | bytes 2228224 | tf_op jit(solution)/shard_map/all_gather | solution.py:168
  6.5 2.8 %copy-start = (f32[16,128,256]{2,1,0:T(8,128)S(1)}, f32[16,128,256]{2,1,0:T(8,128)}, u32[]{:S(2)}) copy-start(f32[16,128,256]{2,1,0:T(8,128)} %param.19) | copy-start | bytes 6291460
  9.4 6.3 %copy-start.4 = (s32[256]{0:T(256)S(1)}, s32[256]{0:T(256)}, u32[]{:S(2)}) copy-start(s32[256]{0:T(256)} %param.20) | copy-start | bytes 3076
  9.4 6.3 %copy-start.5 = (f32[3]{0:T(128)S(1)}, f32[3]{0:T(128)}, u32[]{:S(2)}) copy-start(f32[3]{0:T(128)} %constant.218.clone) | copy-start | bytes 40
  9.4 6.6 %copy-start.7 = (f32[3]{0:T(128)S(1)}, f32[3]{0:T(128)}, u32[]{:S(2)}) copy-start(f32[3]{0:T(128)} %constant.221.clone) | copy-start | bytes 40
  9.4 6.8 %copy-start.6 = (pred[15]{0:T(512)(128)(4,1)S(1)}, pred[15]{0:T(512)(128)(4,1)}, u32[]{:S(2)}) copy-start(pred[15]{0:T(512)(128)(4,1)} %constant.216.clone.1) | copy-start | bytes 49
  9.5 6.7 %collective-permute-start = (f32[2,16,1,256]{3,1,2,0:T(8,128)S(1)}, f32[2,16,1,256]{3,1,2,0:T(8,128)S(1)}, u32[]{:S(2)}, u32[]{:S(2)}) collective-permute-start(f32[2,16,1,256]{3,1,2,0:T(8,128)S(1)} %copy.50), channel_id=1, source_target_pairs={{0,4},{4,8},{8,12},{12,16},{16,20},{20,24},{24,28},{1,5},{5,9},{9,... | collective-permute-start | bytes 98312 | tf_op jit(solution)/shard_map/ppermute | solution.py:21
  14.3 5.3 %collective-permute-start.1 = (f32[2,16,1,256]{3,1,2,0:T(8,128)S(1)}, f32[2,16,1,256]{3,1,2,0:T(8,128)S(1)}, u32[]{:S(2)}, u32[]{:S(2)}) collective-permute-start(f32[2,16,1,256]{3,1,2,0:T(8,128)S(1)} %copy.51), channel_id=1, source_target_pairs={{4,0},{8,4},{12,8},{16,12},{20,16},{24,20},{28,24},{5,1},{9,5},{13... | collective-permute-start | bytes 98312 | tf_op jit(solution)/shard_map/ppermute | solution.py:22
  25.7 8.6 %collective-permute-start.2 = (f32[2,16,130,1]{2,1,3,0:T(8,128)S(1)}, f32[2,16,130,1]{2,1,3,0:T(8,128)S(1)}, u32[]{:S(2)}, u32[]{:S(2)}) collective-permute-start(f32[2,16,130,1]{2,1,3,0:T(8,128)S(1)} %copy.54), channel_id=1, source_target_pairs={{0,1},{1,2},{2,3},{4,5},{5,6},{6,7},{8,9},{9,10},{10,11},{12,13},{... | collective-permute-start | bytes 49928 | tf_op jit(solution)/shard_map/ppermute | solution.py:21
  31.6 4.8 %collective-permute-start.3 = (f32[2,16,130,1]{2,1,3,0:T(8,128)S(1)}, f32[2,16,130,1]{2,1,3,0:T(8,128)S(1)}, u32[]{:S(2)}, u32[]{:S(2)}) collective-permute-start(f32[2,16,130,1]{2,1,3,0:T(8,128)S(1)} %copy.55), channel_id=1, source_target_pairs={{1,0},{2,1},{3,2},{5,4},{6,5},{7,6},{9,8},{10,9},{11,10},{13,12},{... | collective-permute-start | bytes 49928 | tf_op jit(solution)/shard_map/ppermute | solution.py:22
  45.0 1.6 copy-start.1
  51.2 2.2 copy-start.2
  71.5 1.3 copy-start.3
  90.3 8.8 %collective-permute-start.6 = (f32[128,256]{1,0:T(8,128)S(1)}, f32[128,256]{1,0:T(8,128)S(1)}, u32[]{:S(2)}, u32[]{:S(2)}) collective-permute-start(f32[128,256]{1,0:T(8,128)S(1)} %slice_bitcast_fusion.2), channel_id=1, source_target_pairs={{32,0},{64,32},{96,64},{128,96},{160,128},{192,160},{224,192},{256... | collective-permute-start | bytes 393224 | tf_op jit(solution)/shard_map/ppermute | solution.py:30
  102.8 22.0 %collective-permute-start.5 = (f32[128]{0:T(128)S(1)}, f32[128]{0:T(128)S(1)}, u32[]{:S(2)}, u32[]{:S(2)}) collective-permute-start(f32[128]{0:T(128)S(1)} %get-tuple-element.785), channel_id=1, source_target_pairs={{32,0},{64,32},{96,64},{128,96},{160,128},{192,160},{224,192},{256... | collective-permute-start | bytes 1544 | tf_op jit(solution)/shard_map/ppermute | solution.py:30
  122.7 19.5 %collective-permute-start.4 = (f32[128]{0:T(128)S(1)}, f32[128]{0:T(128)S(1)}, u32[]{:S(2)}, u32[]{:S(2)}) collective-permute-start(f32[128]{0:T(128)S(1)} %slice_bitcast_fusion.4), channel_id=1, source_target_pairs={{32,0},{64,32},{96,64},{128,96},{160,128},{192,160},{224,192},{256... | collective-permute-start | bytes 1544 | tf_op jit(solution)/shard_map/ppermute | solution.py:30
Sparse Core Ops, SparseCore 0:
  102.2 44.5 all-gather.7
where the time goes:
time: 230 us; the launch traced here: 227 us
  other arithmetic  108 us (47%)
  blocking collectives  50.1 us (22%)
  local copies, waits for them, and re-layouts  27.9 us (12%)
  starting transfers between devices  19.5 us (8%)
  between operations  13.8 us (6%)
  waiting for transfers between devices  6.55 us (3%)
    dynamic_update_slice x62, other arithmetic, thomas_solve(): lax.scan(forward, start_state, (below_link, diagonal, above_link, tuple(r...  83.6 us
    all_gather x1, blocking collectives, per_device(): lax.all_gather(red_below[None], 'stack', axis=0, tiled=True)  18 us
    all_gather x1, blocking collectives, per_device(): lax.all_gather(red_above[None], 'stack', axis=0, tiled=True)  16.1 us
    all_gather x1, blocking collectives, per_device(): lax.all_gather(red_diag[None], 'stack', axis=0, tiled=True)  16 us
    ppermute x3, starting transfers between devices, from_behind(): lax.ppermute(value, axis, [(source, source + steps) for source in range(f...  9 us
    ppermute x2, starting transfers between devices, with_halo(): before = lax.ppermute(last, axis, up)  7.93 us
    concatenate x2, other arithmetic, with_halo(): x = jnp.concatenate([before, x, after], axis=dim)  6.85 us
    slice x3, local copies, waits for them, and re-layouts, with_halo(): last = lax.slice_in_dim(x, length - width, length, axis=dim)  5.58 us
  transfers between devices with their start and end apart: 8, of which 2 were waited for; matrix products, arithmetic and copies ran while one was open for 5% of the time, Pallas kernels for 0%

commit v1 on v0

v1 whole, which is shorter than its diff:
```python
import functools

import jax
import jax.numpy as jnp
from jax import lax
from jax.experimental import pallas as pl
from jax.experimental.pallas import tpu as pltpu
from jax.sharding import PartitionSpec as P

STACK_K = (0.15, 0.25, 1.0)
PLANE_K = ((0.35, 0.5, 0.7, 0.9), (0.3, 0.45, 0.65, 0.85), (0.8, 0.9, 1.0, 0.95))
FILM = ((0.4, 0.8, 1.2, 1.6), (0.3, 0.6, 1.0, 1.4), (0.0, 0.0, 0.0, 0.0))
LEVEL = (1.5, -1.0, 0.0)
INPLANE = 0.24
STACK_SCALE = 0.2
MESH = pl.DeviceIdType.MESH
SUB = 8
LANES = 128


def face(a, b):
    return 2.0 * a * b / (a + b)


def pick_scalar(code, values):
    out = jnp.float32(values[-1])
    for i in range(len(values) - 2, -1, -1):
        out = jnp.where(code == i, jnp.float32(values[i]), out)
    return out


def pick_pair(index, table):
    flat = [v for row in table for v in row]
    out = jnp.full(index.shape, flat[-1], jnp.float32)
    for i in range(len(flat) - 2, -1, -1):
        if flat[i] != flat[-1]:
            out = jnp.where(index == i, jnp.float32(flat[i]), out)
    return out


def link(scale, first, second):
    rows = []
    for a in STACK_K:
        rows.append(pick_scalar(second, [scale * face(a, b) for b in STACK_K]))
    return jnp.where(first == 0, rows[0], jnp.where(first == 1, rows[1], rows[2]))


def lane(tile, q, width):
    return jnp.broadcast_to(tile[:, q : q + 1], (tile.shape[0], width))


def kernel(
    dims,
    cat_ref,
    corr_ref,
    t_hbm,
    out_ref,
    tbuf,
    e_own,
    e_left,
    e_right,
    corr_dn,
    corr_up,
    cbuf,
    ct,
    ct_rx,
    ld_tx,
    ld_rx,
    sol_tx,
    sol_rx,
    piv,
    t_sem,
    halo_send,
    halo_recv,
    ct_send,
    ct_recv,
    ld_send,
    ld_recv,
    sol_send,
    sol_recv,
):
    ns, nf, nw, nl, nr, nc, scale = dims
    tiles = nr // SUB
    me, fi, wi = lax.axis_index("stack"), lax.axis_index("flow"), lax.axis_index("width")
    f_next, f_prev = lax.rem(fi + 1, nf), lax.rem(fi + nf - 1, nf)
    w_next, w_prev = lax.rem(wi + 1, nw), lax.rem(wi + nw - 1, nw)
    base = me * nl
    half = ns // 2

    load = pltpu.make_async_copy(t_hbm, tbuf.at[:, pl.ds(SUB, nr), :], t_sem)
    load.start()

    barrier = pltpu.get_barrier_semaphore()
    for dev in ({"flow": f_next}, {"flow": f_prev}, {"width": w_next}, {"width": w_prev}):
        pl.semaphore_signal(barrier, inc=1, device_id=dev, device_id_type=MESH)

    @pl.loop(1, ns)
    def _(i):
        pl.semaphore_signal(
            barrier, inc=1, device_id={"stack": lax.rem(me + i, ns)}, device_id_type=MESH
        )

    pl.semaphore_wait(barrier, ns - 1 + 4)

    def remote(src, dst, k, dev):
        return pltpu.make_async_remote_copy(
            src_ref=src,
            dst_ref=dst,
            send_sem=halo_send.at[k],
            recv_sem=halo_recv.at[k],
            device_id=dev,
            device_id_type=MESH,
        )

    row_dn = remote(t_hbm.at[:, pl.ds(nr - SUB, SUB), :], tbuf.at[:, pl.ds(0, SUB), :], 0, {"flow": f_next})
    row_up = remote(t_hbm.at[:, pl.ds(0, SUB), :], tbuf.at[:, pl.ds(nr + SUB, SUB), :], 1, {"flow": f_prev})
    cor_dn = remote(corr_ref, corr_dn, 2, {"flow": f_next})
    cor_up = remote(corr_ref, corr_up, 3, {"flow": f_prev})
    for copy in (cor_dn, cor_up, row_dn, row_up):
        copy.start()

    layer = lax.broadcasted_iota(jnp.int32, (nl, nr), 0)
    column = lax.broadcasted_iota(jnp.int32, (nl, nr), 1)
    cats = [cat_ref[base + j] for j in range(nl)]
    catv = jnp.zeros((nl, nr), jnp.int32)
    for j in range(nl):
        catv = jnp.where(layer == j, cats[j], catv)
    corr = corr_ref[...]
    kind = catv * 4 + corr
    k_own = pick_pair(kind, PLANE_K)
    film = pick_pair(kind, FILM)
    level = jnp.where(catv == 0, LEVEL[0], jnp.where(catv == 1, LEVEL[1], LEVEL[2]))
    mass = 1.0 + film
    links = [link(scale, cats[j], cats[j + 1]) for j in range(nl - 1)]
    m = [mass[j : j + 1, :] for j in range(nl)]
    one, zero = jnp.ones((1, nr), jnp.float32), jnp.zeros((1, nr), jnp.float32)
    phi_ratio, psi_ratio = [None] * nl, [None] * nl
    up = m[nl - 2] + links[nl - 2]
    dn = m[1] + links[0]
    for j in range(nl - 2, 0, -1):
        inv = 1.0 / (up + links[j - 1])
        phi_ratio[j] = links[j - 1] * inv
        if j > 1:
            up = m[j - 1] + links[j - 1] * (up * inv)
        i = nl - 1 - j
        inv = 1.0 / (dn + links[i])
        psi_ratio[i] = links[i] * inv
        if i < nl - 2:
            dn = m[i + 1] + links[i] * (dn * inv)
    phi, psi = [one] + [None] * (nl - 2) + [zero], [zero] + [None] * (nl - 2) + [one]
    for j in range(1, nl - 1):
        phi[j] = phi[j - 1] * phi_ratio[j]
        i = nl - 1 - j
        psi[i] = psi[i + 1] * psi_ratio[i]
    gamma = links[0] * psi[1]
    g_a, g_b = m[0], m[nl - 1]
    for j in range(1, nl - 1):
        g_a = g_a + phi[j] * m[j]
        g_b = g_b + psi[j] * m[j]
    for j in range(nl):
        cbuf[j : j + 1, :] = phi[j]
        cbuf[nl + j : nl + j + 1, :] = psi[j]
    cbuf[5 * nl : 6 * nl, :] = film * level
    cbuf[6 * nl : 6 * nl + 1, :] = g_a
    cbuf[6 * nl + 1 : 6 * nl + 2, :] = g_b
    cbuf[6 * nl + 2 : 6 * nl + 3, :] = gamma
    cbuf[6 * nl + 3 : 6 * nl + 4, :] = 1.0 / gamma
    cbuf[6 * nl + 4 : LANES, :] = jnp.zeros((LANES - 6 * nl - 4, nr), jnp.float32)

    load.wait()
    slot = lax.broadcasted_iota(jnp.int32, (SUB, LANES), 1)

    @pl.loop(0, tiles)
    def _(rt):
        acc = jnp.zeros((SUB, LANES), jnp.float32)
        r = pl.multiple_of(rt * SUB, SUB)
        r1 = pl.multiple_of(r + SUB, SUB)
        for j in range(nl):
            acc = jnp.where(slot == j, lane(tbuf[j, pl.ds(r1, SUB), 0:LANES], 0, LANES), acc)
            acc = jnp.where(
                slot == nl + j,
                lane(tbuf[j, pl.ds(r1, SUB), nc - LANES : nc], LANES - 1, LANES),
                acc,
            )
        e_own[pl.ds(r, SUB), :] = acc

    edge_r = remote(e_own, e_left, 4, {"width": w_next})
    edge_l = remote(e_own, e_right, 5, {"width": w_prev})
    edge_r.start()
    edge_l.start()

    cor_dn.wait_recv()
    cor_up.wait_recv()
    k_dn = pick_pair(catv * 4 + corr_dn[...], PLANE_K)
    k_up = pick_pair(catv * 4 + corr_up[...], PLANE_K)
    last = column == nr - 1
    first = column == 0
    k_after = jnp.where(last, pltpu.roll(k_up, nr - 1, 1), pltpu.roll(k_own, nr - 1, 1))
    k_before = jnp.where(first, pltpu.roll(k_dn, 1, 1), pltpu.roll(k_own, 1, 1))
    c_up = INPLANE * face(k_own, k_after)
    c_dn = INPLANE * face(k_own, k_before)
    c_up = jnp.where(jnp.logical_and(last, fi == nf - 1), 0.0, c_up)
    c_dn = jnp.where(jnp.logical_and(first, fi == 0), 0.0, c_dn)
    cbuf[2 * nl : 3 * nl, :] = c_up
    cbuf[3 * nl : 4 * nl, :] = c_dn
    cbuf[4 * nl : 5 * nl, :] = INPLANE * k_own
    ct[...] = jnp.transpose(cbuf[...])

    def to_stack(src, dst, send, recv, dev):
        return pltpu.make_async_remote_copy(
            src_ref=src,
            dst_ref=dst.at[me],
            send_sem=send.at[dev],
            recv_sem=recv.at[me],
            device_id={"stack": dev},
            device_id_type=MESH,
        )

    @pl.loop(0, ns)
    def _(i):
        dev = lax.rem(me + half + i, ns)
        rows = ct.at[pl.ds(pl.multiple_of(dev * SUB, SUB), SUB), :]

        @pl.when(dev != me)
        def _():
            to_stack(rows, ct_rx, ct_send, ct_recv, dev).start()

        @pl.when(dev == me)
        def _():
            ct_rx[me] = rows[...]

    row_dn.wait_recv()
    row_up.wait_recv()
    edge_r.wait_recv()
    edge_l.wait_recv()

    wide = lax.broadcasted_iota(jnp.int32, (SUB, nc), 1)
    at_first, at_last = wide == 0, wide == nc - 1
    height = lax.broadcasted_iota(jnp.int32, (SUB, nc), 0)
    bottom, top = height == 0, height == SUB - 1

    @pl.loop(0, ns)
    def _(i):
        rt = lax.rem(me + half + i, ns)
        r = pl.multiple_of(rt * SUB, SUB)
        r1, r2 = pl.multiple_of(r + SUB, SUB), pl.multiple_of(r + 2 * SUB, SUB)
        co = ct[pl.ds(r, SUB), :]
        own = e_own[pl.ds(r, SUB), :]
        left = jnp.where(wi > 0, e_left[pl.ds(r, SUB), :], pltpu.roll(own, nl, 1))
        right = jnp.where(wi < nw - 1, e_right[pl.ds(r, SUB), :], pltpu.roll(own, LANES - nl, 1))
        rhs = []
        for j in range(nl):
            t = tbuf[j, pl.ds(r1, SUB), :]
            t_after = jnp.where(bottom, tbuf[j, pl.ds(r2, SUB), :], t)
            t_after = pltpu.roll(t_after, SUB - 1, 0)
            t_before = jnp.where(top, tbuf[j, pl.ds(r, SUB), :], t)
            t_before = pltpu.roll(t_before, 1, 0)
            t_right = jnp.where(at_last, lane(right, j, nc), pltpu.roll(t, nc - 1, 1))
            t_left = jnp.where(at_first, lane(left, nl + j, nc), pltpu.roll(t, 1, 1))
            value = t + lane(co, 2 * nl + j, nc) * (t_after - t)
            value = value + lane(co, 3 * nl + j, nc) * (t_before - t)
            value = value + lane(co, 4 * nl + j, nc) * ((t_right - t) + (t_left - t))
            rhs.append(value + lane(co, 5 * nl + j, nc))
        inv = lane(co, 6 * nl + 3, nc)
        fs = [lane(co, j, nc) for j in range(nl)]
        qs = [lane(co, nl + j, nc) for j in range(nl)]
        run = jnp.zeros((SUB, nc), jnp.float32)
        pre = [run]
        for j in range(1, nl - 1):
            run = run + qs[j] * rhs[j]
            pre.append(run)
        ld_b = run + rhs[nl - 1]
        out_ref[nl - 1, pl.ds(r, SUB), :] = jnp.zeros((SUB, nc), jnp.float32)
        run = jnp.zeros((SUB, nc), jnp.float32)
        for j in range(nl - 2, 0, -1):
            out_ref[j, pl.ds(r, SUB), :] = (fs[j] * pre[j] + qs[j] * run) * inv
            run = run + fs[j] * rhs[j]
        out_ref[0, pl.ds(r, SUB), :] = jnp.zeros((SUB, nc), jnp.float32)
        ld_a = run + rhs[0]

        @pl.when(rt != me)
        def _():
            ld_tx[rt, 0] = ld_a
            ld_tx[rt, 1] = ld_b
            to_stack(ld_tx.at[rt], ld_rx, ld_send, ld_recv, rt).start()

        @pl.when(rt == me)
        def _():
            ld_rx[me, 0] = ld_a
            ld_rx[me, 1] = ld_b

    def wait_from(dst, send, recv, dev):
        pltpu.make_async_remote_copy(
            src_ref=dst.at[dev],
            dst_ref=dst.at[dev],
            send_sem=send.at[dev],
            recv_sem=recv.at[dev],
            device_id={"stack": dev},
            device_id_type=MESH,
        ).wait_recv()

    @pl.loop(1, ns)
    def _(i):
        wait_from(ct_rx, ct_send, ct_recv, lax.rem(me + i, ns))

    ends = [(cat_ref[nl * d + nl - 1], cat_ref[nl * d + nl]) for d in range(ns - 1)]
    s = None
    for d in range(ns):
        co = ct_rx[d]
        g_lo, g_hi, gam = (lane(co, 6 * nl + q, LANES) for q in range(3))
        s = g_lo if d == 0 else g_lo + hold * s
        inv = 1.0 / (s + gam)
        piv[2 * d, 0] = inv
        hold = gam * inv
        piv[2 * d, 1] = hold
        s = g_hi + hold * s
        if d < ns - 1:
            outer = link(scale, *ends[d])
            inv = 1.0 / (s + outer)
            hold = outer * inv
        else:
            inv = 1.0 / s
            hold = jnp.zeros_like(inv)
        piv[2 * d + 1, 0] = inv
        piv[2 * d + 1, 1] = hold

    @pl.loop(1, ns)
    def _(i):
        wait_from(ld_rx, ld_send, ld_recv, lax.rem(me + i, ns))

    def spread(n, q):
        tile = piv[n, q]
        return jnp.concatenate([tile] * (nc // LANES), axis=1)

    flow = []
    for n in range(2 * ns):
        now = ld_rx[n // 2, n % 2]
        if n > 0:
            now = now + spread(n - 1, 1) * flow[n - 1]
        flow.append(now)
    x = None
    for n in range(2 * ns - 1, -1, -1):
        x = flow[n] * spread(n, 0) + (0.0 if x is None else spread(n, 1) * x)
        sol_tx[n // 2, n % 2] = x

    @pl.loop(0, ns)
    def _(i):
        dev = lax.rem(me + half + i, ns)

        @pl.when(dev != me)
        def _():
            to_stack(sol_tx.at[dev], sol_rx, sol_send, sol_recv, dev).start()

        @pl.when(dev == me)
        def _():
            sol_rx[me] = sol_tx[me]

    @pl.loop(0, ns)
    def _(i):
        rt = lax.rem(me + i, ns)

        @pl.when(rt != me)
        def _():
            wait_from(sol_rx, sol_send, sol_recv, rt)

        r = pl.multiple_of(rt * SUB, SUB)
        co = ct[pl.ds(r, SUB), :]
        lo, hi = sol_rx[rt, 0], sol_rx[rt, 1]
        for j in range(nl):
            old = out_ref[j, pl.ds(r, SUB), :]
            out_ref[j, pl.ds(r, SUB), :] = old + (lane(co, j, nc) * lo + lane(co, nl + j, nc) * hi)

    for copy in (row_dn, row_up, cor_dn, cor_up, edge_r, edge_l):
        copy.wait_send()

    @pl.loop(1, ns)
    def _(i):
        dev = lax.rem(me + i, ns)
        rows = ct.at[pl.ds(pl.multiple_of(dev * SUB, SUB), SUB), :]
        to_stack(rows, ct_rx, ct_send, ct_recv, dev).wait_send()
        to_stack(ld_tx.at[dev], ld_rx, ld_send, ld_recv, dev).wait_send()
        to_stack(sol_tx.at[dev], sol_rx, sol_send, sol_recv, dev).wait_send()


def per_device(initial_thermal_state, plate_fluid_category, corrugation_type_grid):
    nl, nr, nc = initial_thermal_state.shape
    ns, nf, nw = lax.axis_size("stack"), lax.axis_size("flow"), lax.axis_size("width")
    total = nl * ns
    scale = STACK_SCALE * float(total * total)
    dims = (ns, nf, nw, nl, nr, nc, scale)
    f32 = jnp.float32
    return pl.pallas_call(
        functools.partial(kernel, dims),
        out_shape=jax.ShapeDtypeStruct((nl, nr, nc), f32),
        in_specs=[
            pl.BlockSpec(memory_space=pltpu.SMEM),
            pl.BlockSpec(memory_space=pltpu.VMEM),
            pl.BlockSpec(memory_space=pl.ANY),
        ],
        out_specs=pl.BlockSpec(memory_space=pltpu.VMEM),
        scratch_shapes=[
            pltpu.VMEM((nl, nr + 2 * SUB, nc), f32),
            pltpu.VMEM((nr, LANES), f32),
            pltpu.VMEM((nr, LANES), f32),
            pltpu.VMEM((nr, LANES), f32),
            pltpu.VMEM((nl, nr), jnp.int32),
            pltpu.VMEM((nl, nr), jnp.int32),
            pltpu.VMEM((LANES, nr), f32),
            pltpu.VMEM((nr, LANES), f32),
            pltpu.VMEM((ns, SUB, LANES), f32),
            pltpu.VMEM((ns, 2, SUB, nc), f32),
            pltpu.VMEM((ns, 2, SUB, nc), f32),
            pltpu.VMEM((ns, 2, SUB, nc), f32),
            pltpu.VMEM((ns, 2, SUB, nc), f32),
            pltpu.VMEM((2 * ns, 2, SUB, LANES), f32),
            pltpu.SemaphoreType.DMA,
            pltpu.SemaphoreType.DMA((6,)),
            pltpu.SemaphoreType.DMA((6,)),
        ]
        + [pltpu.SemaphoreType.DMA((ns,))] * 6,
        compiler_params=pltpu.CompilerParams(collective_id=0, has_side_effects=True),
        name="stack_step",
    )(plate_fluid_category, corrugation_type_grid, initial_thermal_state)


def solution(mesh):
    placed = (P("stack", "flow", "width"), P(), P("stack", "flow"))
    return jax.shard_map(
        per_device,
        mesh=mesh,
        in_specs=placed,
        out_specs=P("stack", "flow", "width"),
        check_vma=False,
    )
```

time: 230 us -> 47.6 us (0.21); the launches traced: 227 us -> 47.4 us
  other arithmetic: 108 us -> 0 us
  blocking collectives: 50.1 us -> 0 us
  Pallas kernels: 0 us -> 44.3 us
  local copies, waits for them, and re-layouts: 27.9 us -> 3.1 us
  starting transfers between devices: 19.5 us -> 0 us
  between operations: 13.8 us -> 0.01 us
  waiting for transfers between devices: 6.55 us -> 0 us
    dynamic_update_slice x62 -> x0, other arithmetic: 83.6 us -> none  [thomas_solve(): lax.scan(forward, start_state, (below_link, diagonal, above_link, tuple(r...]
    all_gather x3 -> x0, blocking collectives: 50.1 us -> none  [the longest x1 18 us: per_device(): lax.all_gather(red_below[None], 'stack', axis=0, tiled=True)]
    pallas_call x0 -> x1, Pallas kernels: none -> 44.3 us  [per_device(): pl.pallas_call(functools.partial(kernel, dims), out_shape=jax.ShapeDtypeS...]
    ppermute x7 -> x0, starting transfers between devices: 19.5 us -> none  [the longest x3 9 us: from_behind(): lax.ppermute(value, axis, [(source, source + steps) for source in range(f...]
    slice x8 -> x0, local copies, waits for them, and re-layouts: 11.4 us -> none  [the longest x3 5.58 us: with_halo(): last = lax.slice_in_dim(x, length - width, length, axis=dim)]
    add x33 -> x0, other arithmetic: 8.87 us -> none  [the longest x1 4.67 us: per_device(): initial_thermal_state + inplane_update * stack_heat_flux]
    concatenate x4 -> x0, other arithmetic: 8.4 us -> none  [the longest x2 6.85 us: with_halo(): x = jnp.concatenate([before, x, after], axis=dim)]
    ppermute x7 -> x0, waiting for transfers between devices: 6.53 us -> none  [the longest x2 3.35 us: with_halo(): after = lax.ppermute(first, axis, down)]
  transfers between devices with their start and end apart: 8 -> 0, of which waited for: 2 -> 0; matrix products, arithmetic and copies ran while one was open for 5% -> 0% of each run, Pallas kernels for 0% -> 0%
where the time goes in v1:
time: 47.6 us; the launch traced here: 47.4 us
  Pallas kernels  44.3 us (93%)
  local copies, waits for them, and re-layouts  3.1 us (7%)
    pallas_call x1, Pallas kernels, per_device(): pl.pallas_call(functools.partial(kernel, dims), out_shape=jax.ShapeDtypeS...  44.3 us
    unnamed x1, local copies, waits for them, and re-layouts  3.1 us

profile of v1, /device:TPU:1, one launch (start us, length us, event | category | flops | bytes accessed | tf_op | source)
XLA Modules:
  0.0 47.4 jit_solution(5082635156654315925)
XLA Ops:
  0.0 44.3 %stack_step.1 = f32[16,128,256]{2,1,0:T(8,128)} custom-call(s32[256]{0:T(256)} %cat_ref.1, s32[16,128]{1,0:T(8,128)} %corr_ref.1, f32[16,128,256]{2,1,0:T(8,128)} %t_hbm.1), custom_call_target="tpu_custom_call" | custom-call | tf_op jit(solution)/shard_map/stack_step/pallas_call | solution.py:392
  44.3 3.1 %copy.5 = f32[16,128,256]{2,1,0:T(8,128)} copy(f32[16,128,256]{2,1,0:T(8,128)} %stack_step.1) | data formatting | bytes 4194304

commit v2 on v1

v2 whole, which is shorter than its diff:
```python
import functools

import jax
import jax.numpy as jnp
from jax import lax
from jax.experimental import pallas as pl
from jax.experimental.pallas import tpu as pltpu
from jax.sharding import PartitionSpec as P

STACK_K = (0.15, 0.25, 1.0)
PLANE_K = ((0.35, 0.5, 0.7, 0.9), (0.3, 0.45, 0.65, 0.85), (0.8, 0.9, 1.0, 0.95))
FILM = ((0.4, 0.8, 1.2, 1.6), (0.3, 0.6, 1.0, 1.4), (0.0, 0.0, 0.0, 0.0))
LEVEL = (1.5, -1.0, 0.0)
INPLANE = 0.24
STACK_SCALE = 0.2
MESH = pl.DeviceIdType.MESH
SUB = 8
LANES = 128
PACK = 4
VMEM_BYTES = 67043328


def face(a, b):
    return 2.0 * a * b / (a + b)


def pick_scalar(code, values):
    out = jnp.float32(values[-1])
    for i in range(len(values) - 2, -1, -1):
        out = jnp.where(code == i, jnp.float32(values[i]), out)
    return out


def pick_pair(index, table):
    flat = [v for row in table for v in row]
    out = jnp.full(index.shape, flat[-1], jnp.float32)
    for i in range(len(flat) - 2, -1, -1):
        if flat[i] != flat[-1]:
            out = jnp.where(index == i, jnp.float32(flat[i]), out)
    return out


def link(scale, first, second):
    rows = []
    for a in STACK_K:
        rows.append(pick_scalar(second, [scale * face(a, b) for b in STACK_K]))
    return jnp.where(first == 0, rows[0], jnp.where(first == 1, rows[1], rows[2]))


def lane(tile, q):
    return jnp.broadcast_to(tile[:, q : q + 1], (tile.shape[0], LANES))


def rows_of(tile):
    return pl.ds(pl.multiple_of(tile * SUB, SUB), SUB)


def kernel(
    dims,
    cat_ref,
    corr_ref,
    t_hbm,
    out_ref,
    tbuf,
    row_lo,
    row_hi,
    e_own,
    e_left,
    e_right,
    corr_dn,
    corr_up,
    comp_tx,
    comp_rx,
    cbuf,
    ct,
    ct_rx,
    bc,
    fold,
    pair_tx,
    pair_rx,
    inner,
    ld_tx,
    ld_rx,
    sol_tx,
    sol_rx,
    end_tx,
    ends_buf,
    piv,
    t_sem,
    near_send,
    near_recv,
    ct_send,
    ct_recv,
    pair_send,
    pair_recv,
    ld_send,
    ld_recv,
    sol_send,
    sol_recv,
    end_send,
    end_recv,
    ready,
):
    ns, nf, nw, nl, nr, nc, scale = dims
    nch, tiles, halves = ns // 2, nr // SUB, nc // LANES
    half = nch // 2
    me, fi, wi = lax.axis_index("stack"), lax.axis_index("flow"), lax.axis_index("width")
    chip, core = me // 2, lax.rem(me, 2)
    other = 1 - core
    partner = {"stack": 2 * chip + other}
    f_next, f_prev = {"flow": lax.rem(fi + 1, nf)}, {"flow": lax.rem(fi + nf - 1, nf)}
    w_next, w_prev = {"width": lax.rem(wi + 1, nw)}, {"width": lax.rem(wi + nw - 1, nw)}

    def at_chip(steps):
        return {"stack": lax.rem(me + 2 * (steps % nch), ns)}

    load = pltpu.make_async_copy(t_hbm, tbuf.at[:, pl.ds(SUB, nr), :], t_sem)
    load.start()

    barrier = pltpu.get_barrier_semaphore()
    near = (f_next, f_prev, w_next, w_prev, partner, at_chip(1), at_chip(-1))
    for dev in near:
        pl.semaphore_signal(barrier, inc=1, device_id=dev, device_id_type=MESH)

    def remote(src, dst, k, dev):
        return pltpu.make_async_remote_copy(
            src_ref=src,
            dst_ref=dst,
            send_sem=near_send.at[k],
            recv_sem=near_recv.at[k],
            device_id=dev,
            device_id_type=MESH,
        )

    layer = lax.broadcasted_iota(jnp.int32, (nl, nr), 0)
    column = lax.broadcasted_iota(jnp.int32, (nl, nr), 1)
    base = me * nl
    cats = [cat_ref[base + j] for j in range(nl)]
    catv = jnp.zeros((nl, nr), jnp.int32)
    for j in range(nl):
        catv = jnp.where(layer == j, cats[j], catv)
    kind = catv * 4 + corr_ref[...]
    k_own = pick_pair(kind, PLANE_K)
    film = pick_pair(kind, FILM)
    level = jnp.where(catv == 0, LEVEL[0], jnp.where(catv == 1, LEVEL[1], LEVEL[2]))
    mass = 1.0 + film
    links = [link(scale, cats[j], cats[j + 1]) for j in range(nl - 1)]
    m = [mass[j : j + 1, :] for j in range(nl)]
    one, zero = jnp.ones((1, nr), jnp.float32), jnp.zeros((1, nr), jnp.float32)
    phi_ratio, psi_ratio = [None] * nl, [None] * nl
    up = m[nl - 2] + links[nl - 2]
    dn = m[1] + links[0]
    for j in range(nl - 2, 0, -1):
        inv = 1.0 / (up + links[j - 1])
        phi_ratio[j] = links[j - 1] * inv
        if j > 1:
            up = m[j - 1] + links[j - 1] * (up * inv)
        i = nl - 1 - j
        inv = 1.0 / (dn + links[i])
        psi_ratio[i] = links[i] * inv
        if i < nl - 2:
            dn = m[i + 1] + links[i] * (dn * inv)
    phi, psi = [one] + [None] * (nl - 2) + [zero], [zero] + [None] * (nl - 2) + [one]
    for j in range(1, nl - 1):
        phi[j] = phi[j - 1] * phi_ratio[j]
        i = nl - 1 - j
        psi[i] = psi[i + 1] * psi_ratio[i]
    gamma = links[0] * psi[1]
    g_a, g_b = m[0], m[nl - 1]
    for j in range(1, nl - 1):
        g_a = g_a + phi[j] * m[j]
        g_b = g_b + psi[j] * m[j]
    comp_tx[0:1, :] = g_a
    comp_tx[1:2, :] = g_b
    comp_tx[2:3, :] = gamma
    comp_tx[3:SUB, :] = jnp.zeros((SUB - 3, nr), jnp.float32)

    pl.semaphore_wait(barrier, len(near))
    comp = remote(comp_tx, comp_rx, 6, partner)
    cor_dn = remote(corr_ref, corr_dn, 2, f_next)
    cor_up = remote(corr_ref, corr_up, 3, f_prev)
    row_dn = remote(t_hbm.at[:, pl.ds(nr - 1, 1), :], row_lo, 0, f_next)
    row_up = remote(t_hbm.at[:, pl.ds(0, 1), :], row_hi, 1, f_prev)
    for copy in (comp, cor_dn, cor_up, row_dn, row_up):
        copy.start()
    for steps in (1, -1):
        pl.semaphore_signal(ready.at[0], inc=1, device_id=at_chip(steps), device_id_type=MESH)

    load.wait()
    slot = lax.broadcasted_iota(jnp.int32, (SUB, LANES), 1)
    at_first, at_last = slot == 0, slot == LANES - 1
    height = lax.broadcasted_iota(jnp.int32, (SUB, LANES), 0)
    bottom, top = height == 0, height == SUB - 1
    span = LANES // PACK

    @pl.loop(0, tiles // PACK)
    def _(g):
        acc = [jnp.zeros((SUB, LANES), jnp.float32) for _ in range(2)]
        for side, (start, q) in enumerate(((0, 0), (nc - LANES, LANES - 1))):
            for s in range(PACK):
                r = rows_of(g * PACK + s + 1)
                for j in range(nl):
                    value = lane(tbuf[j, r, start : start + LANES], q)
                    acc[side] = jnp.where(slot == s * span + side * nl + j, value, acc[side])
        e_own[rows_of(g), :] = acc[0] + acc[1]

    edge_r = remote(e_own, e_left, 4, w_next)
    edge_l = remote(e_own, e_right, 5, w_prev)
    edge_r.start()
    edge_l.start()

    pl.semaphore_wait(ready.at[0], 2)
    if nch > 4:
        for steps in (2, -2):
            pl.semaphore_signal(ready.at[1], inc=1, device_id=at_chip(steps), device_id_type=MESH)

    def inplane(k_before, k_after):
        last, first = column == nr - 1, column == 0
        after = jnp.where(last, k_after, pltpu.roll(k_own, nr - 1, 1))
        before = jnp.where(first, k_before, pltpu.roll(k_own, 1, 1))
        c_up = INPLANE * face(k_own, after)
        c_dn = INPLANE * face(k_own, before)
        c_up = jnp.where(jnp.logical_and(last, fi == nf - 1), 0.0, c_up)
        c_dn = jnp.where(jnp.logical_and(first, fi == 0), 0.0, c_dn)
        c_lr = INPLANE * k_own
        cbuf[2 * nl : 3 * nl, :] = c_up
        cbuf[3 * nl : 4 * nl, :] = c_dn
        cbuf[4 * nl : 5 * nl, :] = 1.0 - ((c_up + c_dn) + 2.0 * c_lr)
        return c_lr

    for j in range(nl):
        cbuf[j : j + 1, :] = phi[j]
        cbuf[nl + j : nl + j + 1, :] = psi[j]
    cbuf[5 * nl : 6 * nl, :] = inplane(k_own, k_own)
    cbuf[6 * nl : 7 * nl, :] = film * level

    comp.wait_recv()
    theirs = [comp_rx[q : q + 1, :] for q in range(3)]
    low = [jnp.where(core == 0, a, b) for a, b in zip((g_a, g_b, gamma), theirs)]
    high = [jnp.where(core == 0, b, a) for a, b in zip((g_a, g_b, gamma), theirs)]
    mid = link(scale, cat_ref[2 * nl * chip + nl - 1], cat_ref[2 * nl * chip + nl])
    t_in = high[0] + high[2]
    t_inv = 1.0 / (t_in + mid)
    t_out = low[1] + mid * (t_in * t_inv)
    w_p = low[2] / (low[2] + t_out)
    w_q = w_p * (mid * t_inv)
    s_in = low[1] + low[2]
    s_inv = 1.0 / (s_in + mid)
    s_out = high[0] + mid * (s_in * s_inv)
    w_v = high[2] / (high[2] + s_out)
    w_u = w_v * (mid * s_inv)
    chip_gamma = low[2] * w_u
    chip_lo = low[0] + w_p * low[1] + w_q * high[0]
    chip_hi = high[1] + w_u * low[1] + w_v * high[0]
    extra = (
        1.0 / gamma,
        w_p,
        w_q,
        w_u,
        w_v,
        w_u / chip_gamma,
        w_q / chip_gamma,
        chip_lo,
        chip_hi,
        chip_gamma,
    )
    x0 = 7 * nl
    for q, value in enumerate(extra):
        cbuf[x0 + q : x0 + q + 1, :] = value
    cbuf[x0 + len(extra) : LANES, :] = jnp.zeros((LANES - x0 - len(extra), nr), jnp.float32)
    ct[...] = jnp.transpose(cbuf[...])

    for q in range(x0 + 7):

        @pl.loop(0, tiles, unroll=8 if tiles % 8 == 0 else 4)
        def _(rt):
            bc[q, rt] = lane(ct[rows_of(rt), :], q)

    cor_dn.wait_recv()
    cor_up.wait_recv()
    inplane(
        pltpu.roll(pick_pair(catv * 4 + corr_dn[...], PLANE_K), 1, 1),
        pltpu.roll(pick_pair(catv * 4 + corr_up[...], PLANE_K), nr - 1, 1),
    )
    edge_co = jnp.transpose(cbuf[...])
    for rt in (0, tiles - 1):
        for q in range(2 * nl, 5 * nl):
            bc[q, rt] = lane(edge_co[rt * SUB : rt * SUB + SUB, :], q)

    row_dn.wait_recv()
    row_up.wait_recv()
    for j in range(nl):
        tbuf[j, SUB - 1 : SUB, :] = row_lo[j]
        tbuf[j, nr + SUB : nr + SUB + 1, :] = row_hi[j]
    edge_r.wait_recv()
    edge_l.wait_recv()

    def block(rt):
        g, s = rt // PACK, lax.rem(rt, PACK)
        turn = lax.rem((PACK - s) * span, LANES)
        own = e_own[rows_of(g), :]
        left = jnp.where(wi > 0, e_left[rows_of(g), :], pltpu.roll(own, nl, 1))
        right = jnp.where(wi < nw - 1, e_right[rows_of(g), :], pltpu.roll(own, LANES - nl, 1))
        left, right = pltpu.roll(left, turn, 1), pltpu.roll(right, turn, 1)
        r0, r1, r2 = rows_of(rt), rows_of(rt + 1), rows_of(rt + 2)
        inv = bc[x0, rt]
        pre, run = [None] * halves, [None] * halves
        ld_a, ld_b = [None] * halves, [None] * halves
        for j in range(nl):
            ts = [tbuf[j, r1, h * LANES : (h + 1) * LANES] for h in range(halves)]
            fwd = [pltpu.roll(t, 1, 1) for t in ts]
            bwd = [pltpu.roll(t, LANES - 1, 1) for t in ts]
            from_l = [pltpu.roll(left, LANES - nl - j, 1)] + fwd[:-1]
            from_r = bwd[1:] + [pltpu.roll(right, LANES - 1 - j, 1)]
            f, p = bc[j, rt], bc[nl + j, rt]
            for h in range(halves):
                cols = slice(h * LANES, (h + 1) * LANES)
                t = ts[h]
                after = pltpu.roll(jnp.where(bottom, tbuf[j, r2, cols], t), SUB - 1, 0)
                before = pltpu.roll(jnp.where(top, tbuf[j, r0, cols], t), 1, 0)
                beside = jnp.where(at_first, from_l[h], fwd[h]) + jnp.where(at_last, from_r[h], bwd[h])
                rhs = bc[4 * nl + j, rt] * t + bc[6 * nl + j, rt]
                rhs = rhs + bc[2 * nl + j, rt] * after
                rhs = rhs + bc[3 * nl + j, rt] * before
                rhs = rhs + bc[5 * nl + j, rt] * beside
                if j == 0:
                    ld_a[h] = rhs
                elif j == nl - 1:
                    ld_b[h] = pre[h] + rhs
                else:
                    if j == 1:
                        value = jnp.zeros((SUB, LANES), jnp.float32)
                        pre[h], run[h] = p * rhs, f * rhs
                    else:
                        value = (f * pre[h] - p * run[h]) * inv
                        pre[h], run[h] = pre[h] + p * rhs, run[h] + f * rhs
                    out_ref[j, r0, cols] = value
        for h in range(halves):
            ld_a[h] = ld_a[h] + run[h]
            fold[rt, :, h * LANES : (h + 1) * LANES] = run[h] * inv
        return ld_a, ld_b

    def to_partner(src, dst, send, recv, k):
        return pltpu.make_async_remote_copy(
            src_ref=src.at[k],
            dst_ref=dst.at[k],
            send_sem=send.at[k],
            recv_sem=recv.at[k],
            device_id=partner,
            device_id_type=MESH,
        )

    def to_chip(src, dst, send, recv, k):
        return pltpu.make_async_remote_copy(
            src_ref=src,
            dst_ref=dst.at[chip],
            send_sem=send.at[k],
            recv_sem=recv.at[chip],
            device_id={"stack": 2 * k + core},
            device_id_type=MESH,
        )

    def from_chip(dst, send, recv, k):
        return pltpu.make_async_remote_copy(
            src_ref=dst.at[k],
            dst_ref=dst.at[k],
            send_sem=send.at[k],
            recv_sem=recv.at[k],
            device_id={"stack": 2 * k + core},
            device_id_type=MESH,
        )

    @pl.loop(0, nch)
    def _(i):
        k = lax.rem(chip + half + i, nch)
        ld_a, ld_b = block(2 * k + other)
        for h in range(halves):
            cols = slice(h * LANES, (h + 1) * LANES)
            pair_tx[k, 0, :, cols] = ld_a[h]
            pair_tx[k, 1, :, cols] = ld_b[h]
        to_partner(pair_tx, pair_rx, pair_send, pair_recv, k).start()

    if nch > 4:
        pl.semaphore_wait(ready.at[1], 2)

    @pl.loop(0, nch)
    def _(i):
        k = lax.rem(chip + half + i, nch)
        rows = ct.at[rows_of(2 * k + core), :]

        @pl.when(k != chip)
        def _():
            to_chip(rows, ct_rx, ct_send, ct_recv, k).start()

        @pl.when(k == chip)
        def _():
            ct_rx[k] = rows[...]

    @pl.loop(0, nch)
    def _(i):
        k = lax.rem(chip + half + i, nch)
        rt = 2 * k + core
        ld_a, ld_b = block(rt)
        to_partner(pair_tx, pair_rx, pair_send, pair_recv, k).wait_recv()
        p, q, u, v = (bc[x0 + 1 + n, rt] for n in range(4))
        for h in range(halves):
            cols = slice(h * LANES, (h + 1) * LANES)
            their_a, their_b = pair_rx[k, 0, :, cols], pair_rx[k, 1, :, cols]
            f_b = jnp.where(core == 0, ld_b[h], their_b)
            f_a = jnp.where(core == 0, their_a, ld_a[h])
            f_lo = jnp.where(core == 0, ld_a[h], their_a)
            f_hi = jnp.where(core == 0, their_b, ld_b[h])
            to_lo = p * f_b + q * f_a
            to_hi = u * f_b + v * f_a
            inner[k, 0, :, cols] = to_lo
            inner[k, 1, :, cols] = to_hi
            ld_tx[k, 0, :, cols] = f_lo + to_lo
            ld_tx[k, 1, :, cols] = f_hi + to_hi

        @pl.when(k != chip)
        def _():
            to_chip(ld_tx.at[k], ld_rx, ld_send, ld_recv, k).start()

        @pl.when(k == chip)
        def _():
            ld_rx[k] = ld_tx[k]

    @pl.loop(1, nch)
    def _(i):
        from_chip(ct_rx, ct_send, ct_recv, lax.rem(chip + i, nch)).wait_recv()

    s, hold = None, None
    for d in range(nch):
        g_lo, g_hi, gam = (lane(ct_rx[d], x0 + 7 + q) for q in range(3))
        s = g_lo if d == 0 else g_lo + hold * s
        inv = 1.0 / (s + gam)
        hold = gam * inv
        piv[2 * d, 0], piv[2 * d, 1] = inv, hold
        s = g_hi + hold * s
        if d < nch - 1:
            outer = link(scale, cat_ref[2 * nl * (d + 1) - 1], cat_ref[2 * nl * (d + 1)])
            inv = 1.0 / (s + outer)
            hold = outer * inv
        else:
            inv = 1.0 / s
            hold = jnp.zeros_like(inv)
        piv[2 * d + 1, 0], piv[2 * d + 1, 1] = inv, hold

    @pl.loop(1, nch)
    def _(i):
        from_chip(ld_rx, ld_send, ld_recv, lax.rem(chip + i, nch)).wait_recv()

    for h in range(halves):
        cols = slice(h * LANES, (h + 1) * LANES)
        flow = []
        for n in range(2 * nch):
            now = ld_rx[n // 2, n % 2, :, cols]
            if n > 0:
                now = now + piv[n - 1, 1] * flow[n - 1]
            flow.append(now)
        x = flow[-1] * piv[2 * nch - 1, 0]
        sol_tx[nch - 1, 1, :, cols] = x
        for n in range(2 * nch - 2, -1, -1):
            x = flow[n] * piv[n, 0] + piv[n, 1] * x
            sol_tx[n // 2, n % 2, :, cols] = x

    @pl.loop(0, nch)
    def _(i):
        k = lax.rem(chip + half + i, nch)

        @pl.when(k != chip)
        def _():
            to_chip(sol_tx.at[k], sol_rx, sol_send, sol_recv, k).start()

        @pl.when(k == chip)
        def _():
            sol_rx[k] = sol_tx[k]

    def finish(rt, lo, hi):
        r = rows_of(rt)
        for h in range(halves):
            cols = slice(h * LANES, (h + 1) * LANES)
            out_ref[0, r, cols] = lo[h]
            out_ref[nl - 1, r, cols] = hi[h]
            bent = hi[h] + fold[rt, :, cols]
            for j in range(1, nl - 1):
                ends = bc[j, rt] * lo[h] + bc[nl + j, rt] * bent
                out_ref[j, r, cols] = out_ref[j, r, cols] + ends

    @pl.loop(0, nch)
    def _(i):
        k = lax.rem(chip + i, nch)
        rt = 2 * k + core

        @pl.when(k != chip)
        def _():
            from_chip(sol_rx, sol_send, sol_recv, k).wait_recv()

        p, q, u, v, s_b, s_a = (bc[x0 + 1 + n, rt] for n in range(6))
        lo, hi = [None] * halves, [None] * halves
        for h in range(halves):
            cols = slice(h * LANES, (h + 1) * LANES)
            x_lo, x_hi = sol_rx[k, 0, :, cols], sol_rx[k, 1, :, cols]
            x_b = p * x_lo + u * x_hi + s_b * inner[k, 0, :, cols]
            x_a = q * x_lo + v * x_hi + s_a * inner[k, 1, :, cols]
            lo[h] = jnp.where(core == 0, x_lo, x_a)
            hi[h] = jnp.where(core == 0, x_b, x_hi)
            end_tx[k, 0, :, cols] = jnp.where(core == 0, x_a, x_lo)
            end_tx[k, 1, :, cols] = jnp.where(core == 0, x_hi, x_b)
        to_partner(end_tx, ends_buf, end_send, end_recv, k).start()
        finish(rt, lo, hi)

    @pl.loop(0, nch)
    def _(i):
        k = lax.rem(chip + i, nch)
        to_partner(end_tx, ends_buf, end_send, end_recv, k).wait_recv()
        lo = [ends_buf[k, 0, :, h * LANES : (h + 1) * LANES] for h in range(halves)]
        hi = [ends_buf[k, 1, :, h * LANES : (h + 1) * LANES] for h in range(halves)]
        finish(2 * k + other, lo, hi)

    for copy in (comp, row_dn, row_up, cor_dn, cor_up, edge_r, edge_l):
        copy.wait_send()

    @pl.loop(0, nch)
    def _(k):
        to_partner(pair_tx, pair_rx, pair_send, pair_recv, k).wait_send()
        to_partner(end_tx, ends_buf, end_send, end_recv, k).wait_send()

        @pl.when(k != chip)
        def _():
            to_chip(ct.at[rows_of(2 * k + core), :], ct_rx, ct_send, ct_recv, k).wait_send()
            to_chip(ld_tx.at[k], ld_rx, ld_send, ld_recv, k).wait_send()
            to_chip(sol_tx.at[k], sol_rx, sol_send, sol_recv, k).wait_send()


def copy_out(parts, x_ref, out_ref, sem):
    step = x_ref.shape[0] // parts
    copies = [
        pltpu.make_async_copy(
            x_ref.at[pl.ds(n * step, step)], out_ref.at[pl.ds(n * step, step)], sem.at[n]
        )
        for n in range(parts)
    ]
    for copy in copies:
        copy.start()
    for copy in copies:
        copy.wait()


def per_device(initial_thermal_state, plate_fluid_category, corrugation_type_grid):
    nl, nr, nc = initial_thermal_state.shape
    ns, nf, nw = lax.axis_size("stack"), lax.axis_size("flow"), lax.axis_size("width")
    nch, tiles = ns // 2, nr // SUB
    total = nl * ns
    scale = STACK_SCALE * float(total * total)
    dims = (ns, nf, nw, nl, nr, nc, scale)
    f32 = jnp.float32
    packed = (tiles // PACK * SUB, LANES)
    tile_pair = pltpu.VMEM((nch, 2, SUB, nc), f32)
    dma = pltpu.SemaphoreType.DMA
    result = pl.pallas_call(
        functools.partial(kernel, dims),
        out_shape=pltpu.VMEM((nl, nr, nc), f32),
        in_specs=[
            pl.BlockSpec(memory_space=pltpu.SMEM),
            pl.BlockSpec(memory_space=pltpu.VMEM),
            pl.BlockSpec(memory_space=pl.ANY),
        ],
        out_specs=pl.BlockSpec(memory_space=pltpu.VMEM),
        scratch_shapes=[
            pltpu.VMEM((nl, nr + 2 * SUB, nc), f32),
            pltpu.VMEM((nl, 1, nc), f32),
            pltpu.VMEM((nl, 1, nc), f32),
            pltpu.VMEM(packed, f32),
            pltpu.VMEM(packed, f32),
            pltpu.VMEM(packed, f32),
            pltpu.VMEM((nl, nr), jnp.int32),
            pltpu.VMEM((nl, nr), jnp.int32),
            pltpu.VMEM((SUB, nr), f32),
            pltpu.VMEM((SUB, nr), f32),
            pltpu.VMEM((LANES, nr), f32),
            pltpu.VMEM((nr, LANES), f32),
            pltpu.VMEM((nch, SUB, LANES), f32),
            pltpu.VMEM((7 * nl + 7, tiles, SUB, LANES), f32),
            pltpu.VMEM((tiles, SUB, nc), f32),
        ]
        + [tile_pair] * 9
        + [
            pltpu.VMEM((2 * nch, 2, SUB, LANES), f32),
            dma,
            dma((7,)),
            dma((7,)),
        ]
        + [dma((nch,))] * 10
        + [pltpu.SemaphoreType.REGULAR((2,))],
        compiler_params=pltpu.CompilerParams(
            collective_id=0,
            has_side_effects=True,
            vmem_limit_bytes=VMEM_BYTES - 4 * nl * nr * nc - (1 << 20),
        ),
        name="stack_step",
    )(plate_fluid_category, corrugation_type_grid, initial_thermal_state)
    parts = 4
    return pl.pallas_call(
        functools.partial(copy_out, parts),
        out_shape=jax.ShapeDtypeStruct((nl, nr, nc), f32),
        in_specs=[pl.BlockSpec(memory_space=pltpu.VMEM)],
        out_specs=pl.BlockSpec(memory_space=pl.ANY),
        scratch_shapes=[dma((parts,))],
        compiler_params=pltpu.CompilerParams(vmem_limit_bytes=1 << 20),
        name="copy_out",
    )(result)


def solution(mesh):
    placed = (P("stack", "flow", "width"), P(), P("stack", "flow"))
    return jax.shard_map(
        per_device,
        mesh=mesh,
        in_specs=placed,
        out_specs=P("stack", "flow", "width"),
        check_vma=False,
    )
```

time: 47.6 us -> 52.3 us (1.099)
  Pallas kernels: 44.3 us -> 52.1 us
  local copies, waits for them, and re-layouts: 3.1 us -> 0 us
    pallas_call x1 -> x2, Pallas kernels: 44.3 us -> 52.1 us  [the longest x1 50.7 us: per_device(): pl.pallas_call(functools.partial(kernel, dims), out_shape=pltpu.VMEM((nl,...]
    unnamed x1 -> x0, local copies, waits for them, and re-layouts: 3.1 us -> none
where the time goes in v2:
time: 52.3 us; the launch traced here: 52.1 us
  Pallas kernels  52.1 us (100%)
    pallas_call x1, Pallas kernels, per_device(): pl.pallas_call(functools.partial(kernel, dims), out_shape=pltpu.VMEM((nl,...  50.7 us
    pallas_call x1, Pallas kernels, per_device(): pl.pallas_call(functools.partial(copy_out, parts), out_shape=jax.ShapeDty...  1.35 us

profile of v2, /device:TPU:1, one launch (start us, length us, event | category | flops | bytes accessed | tf_op | source)
XLA Modules:
  0.0 52.1 jit_solution(15016191910510801931)
XLA Ops:
  0.0 50.7 %stack_step.1.x_ref = f32[16,128,256]{2,1,0:T(8,128)S(1)} custom-call(s32[256]{0:T(256)} %cat_ref.1, s32[16,128]{1,0:T(8,128)} %corr_ref.1, f32[16,128,256]{2,1,0:T(8,128)} %t_hbm.1), custom_call_target="tpu_custom_call" | custom-call | tf_op jit(solution)/shard_map/stack_step/pallas_call | solution.py:561
  50.8 1.3 %copy_out.1 = f32[16,128,256]{2,1,0:T(8,128)} custom-call(f32[16,128,256]{2,1,0:T(8,128)S(1)} %stack_step.1.x_ref), custom_call_target="tpu_custom_call" | custom-call | tf_op jit(solution)/shard_map/copy_out/pallas_call | solution.py:604

commit v3 on v2

--- a/solution.py
+++ b/solution.py
@@ -18,6 +18,7 @@
 LANES = 128
 PACK = 4
 VMEM_BYTES = 67043328
+LOADS = 4
 
 
 def face(a, b):
@@ -75,6 +76,7 @@
     ct,
     ct_rx,
     bc,
+    mc,
     fold,
     pair_tx,
     pair_rx,
@@ -114,8 +116,17 @@
     def at_chip(steps):
         return {"stack": lax.rem(me + 2 * (steps % nch), ns)}
 
-    load = pltpu.make_async_copy(t_hbm, tbuf.at[:, pl.ds(SUB, nr), :], t_sem)
-    load.start()
+    part = nl // LOADS
+    loads = [
+        pltpu.make_async_copy(
+            t_hbm.at[pl.ds(n * part, part)],
+            tbuf.at[pl.ds(n * part, part), pl.ds(SUB, nr), :],
+            t_sem.at[n],
+        )
+        for n in range(LOADS)
+    ]
+    for load in loads:
+        load.start()
 
     barrier = pltpu.get_barrier_semaphore()
     near = (f_next, f_prev, w_next, w_prev, partner, at_chip(1), at_chip(-1))
@@ -186,12 +197,14 @@
     for steps in (1, -1):
         pl.semaphore_signal(ready.at[0], inc=1, device_id=at_chip(steps), device_id_type=MESH)
 
-    load.wait()
+    for load in loads:
+        load.wait()
     slot = lax.broadcasted_iota(jnp.int32, (SUB, LANES), 1)
     at_first, at_last = slot == 0, slot == LANES - 1
     height = lax.broadcasted_iota(jnp.int32, (SUB, LANES), 0)
     bottom, top = height == 0, height == SUB - 1
     span = LANES // PACK
+    x0 = 5 * nl + 1
 
     @pl.loop(0, tiles // PACK)
     def _(g):
@@ -200,8 +213,9 @@
             for s in range(PACK):
                 r = rows_of(g * PACK + s + 1)
                 for j in range(nl):
-                    value = lane(tbuf[j, r, start : start + LANES], q)
-                    acc[side] = jnp.where(slot == s * span + side * nl + j, value, acc[side])
+                    to = s * span + side * nl + j
+                    value = pltpu.roll(tbuf[j, r, start : start + LANES], (to - q) % LANES, 1)
+                    acc[side] = jnp.where(slot == to, value, acc[side])
         e_own[rows_of(g), :] = acc[0] + acc[1]
 
     edge_r = remote(e_own, e_left, 4, w_next)
@@ -209,30 +223,33 @@
     edge_r.start()
     edge_l.start()
 
-    pl.semaphore_wait(ready.at[0], 2)
-    if nch > 4:
-        for steps in (2, -2):
-            pl.semaphore_signal(ready.at[1], inc=1, device_id=at_chip(steps), device_id_type=MESH)
-
-    def inplane(k_before, k_after):
-        last, first = column == nr - 1, column == 0
-        after = jnp.where(last, k_after, pltpu.roll(k_own, nr - 1, 1))
-        before = jnp.where(first, k_before, pltpu.roll(k_own, 1, 1))
-        c_up = INPLANE * face(k_own, after)
-        c_dn = INPLANE * face(k_own, before)
-        c_up = jnp.where(jnp.logical_and(last, fi == nf - 1), 0.0, c_up)
-        c_dn = jnp.where(jnp.logical_and(first, fi == 0), 0.0, c_dn)
-        c_lr = INPLANE * k_own
-        cbuf[2 * nl : 3 * nl, :] = c_up
-        cbuf[3 * nl : 4 * nl, :] = c_dn
-        cbuf[4 * nl : 5 * nl, :] = 1.0 - ((c_up + c_dn) + 2.0 * c_lr)
-        return c_lr
-
+    last, first = column == nr - 1, column == 0
+    k_next = pltpu.roll(k_own, nr - 1, 1)
+    c_lr = INPLANE * k_own
     for j in range(nl):
         cbuf[j : j + 1, :] = phi[j]
         cbuf[nl + j : nl + j + 1, :] = psi[j]
-    cbuf[5 * nl : 6 * nl, :] = inplane(k_own, k_own)
-    cbuf[6 * nl : 7 * nl, :] = film * level
+    cbuf[2 * nl : 3 * nl, :] = INPLANE * face(k_own, k_next)
+    cbuf[3 * nl : 4 * nl, :] = c_lr
+    cbuf[4 * nl : 5 * nl, :] = film * level
+    cbuf[5 * nl : 5 * nl + 1, :] = 1.0 / gamma
+    cbuf[5 * nl + 1 : LANES, :] = jnp.zeros((LANES - 5 * nl - 1, nr), jnp.float32)
+    ct[...] = jnp.transpose(cbuf[...])
+
+    @pl.loop(0, tiles // PACK)
+    def _(g):
+        tile = [ct[rows_of(g * PACK + s), :] for s in range(PACK)]
+        for q in range(5 * nl + 1):
+            for s in range(PACK):
+                bc[q, g * PACK + s] = lane(tile[s], q)
+        for j in range(nl):
+            for s in range(PACK):
+                rt = g * PACK + s
+                up = bc[2 * nl + j, rt]
+                before = bc[2 * nl + j, jnp.maximum(rt - 1, 0)]
+                dn = pltpu.roll(jnp.where(top, before, up), 1, 0)
+                bc[x0 + j, rt] = dn
+                bc[x0 + nl + j, rt] = 1.0 - ((up + dn) + 2.0 * bc[3 * nl + j, rt])
 
     comp.wait_recv()
     theirs = [comp_rx[q : q + 1, :] for q in range(3)]
@@ -252,40 +269,36 @@
     chip_gamma = low[2] * w_u
     chip_lo = low[0] + w_p * low[1] + w_q * high[0]
     chip_hi = high[1] + w_u * low[1] + w_v * high[0]
-    extra = (
-        1.0 / gamma,
-        w_p,
-        w_q,
-        w_u,
-        w_v,
-        w_u / chip_gamma,
-        w_q / chip_gamma,
-        chip_lo,
-        chip_hi,
-        chip_gamma,
-    )
-    x0 = 7 * nl
-    for q, value in enumerate(extra):
-        cbuf[x0 + q : x0 + q + 1, :] = value
-    cbuf[x0 + len(extra) : LANES, :] = jnp.zeros((LANES - x0 - len(extra), nr), jnp.float32)
+    merge = (w_p, w_q, w_u, w_v, w_u / chip_gamma, w_q / chip_gamma)
+    for q, value in enumerate(merge + (chip_lo, chip_hi, chip_gamma)):
+        cbuf[q : q + 1, :] = value
     ct[...] = jnp.transpose(cbuf[...])
-
-    for q in range(x0 + 7):
-
-        @pl.loop(0, tiles, unroll=8 if tiles % 8 == 0 else 4)
-        def _(rt):
-            bc[q, rt] = lane(ct[rows_of(rt), :], q)
+    for k in range(nch):
+        tile = ct[rows_of(2 * k + core), :]
+        for q in range(len(merge)):
+            mc[q, k] = lane(tile, q)
 
     cor_dn.wait_recv()
     cor_up.wait_recv()
-    inplane(
-        pltpu.roll(pick_pair(catv * 4 + corr_dn[...], PLANE_K), 1, 1),
-        pltpu.roll(pick_pair(catv * 4 + corr_up[...], PLANE_K), nr - 1, 1),
-    )
-    edge_co = jnp.transpose(cbuf[...])
-    for rt in (0, tiles - 1):
-        for q in range(2 * nl, 5 * nl):
-            bc[q, rt] = lane(edge_co[rt * SUB : rt * SUB + SUB, :], q)
+    k_dn = pick_pair(catv * 4 + corr_dn[...], PLANE_K)
+    k_up = pick_pair(catv * 4 + corr_up[...], PLANE_K)
+    c_dn = INPLANE * face(k_own, pltpu.roll(k_dn, 1, 1))
+    c_up = INPLANE * face(k_own, pltpu.roll(k_up, nr - 1, 1))
+    c_dn = jnp.where(fi == 0, 0.0, jnp.broadcast_to(c_dn[:, 0:1], (nl, LANES)))
+    c_up = jnp.where(fi == nf - 1, 0.0, jnp.broadcast_to(c_up[:, nr - 1 : nr], (nl, LANES)))
+    end = tiles - 1
+    for j in range(nl):
+        dn = jnp.where(bottom, c_dn[j : j + 1, :], bc[x0 + j, 0])
+        bc[x0 + j, 0] = dn
+        up = jnp.where(top, c_up[j : j + 1, :], bc[2 * nl + j, end])
+        bc[2 * nl + j, end] = up
+        bc[x0 + nl + j, 0] = 1.0 - ((bc[2 * nl + j, 0] + dn) + 2.0 * bc[3 * nl + j, 0])
+        bc[x0 + nl + j, end] = 1.0 - ((up + bc[x0 + j, end]) + 2.0 * bc[3 * nl + j, end])
+
+    pl.semaphore_wait(ready.at[0], 2)
+    if nch > 4:
+        for steps in (2, -2):
+            pl.semaphore_signal(ready.at[1], inc=1, device_id=at_chip(steps), device_id_type=MESH)
 
     row_dn.wait_recv()
     row_up.wait_recv()
@@ -303,7 +316,7 @@
         right = jnp.where(wi < nw - 1, e_right[rows_of(g), :], pltpu.roll(own, LANES - nl, 1))
         left, right = pltpu.roll(left, turn, 1), pltpu.roll(right, turn, 1)
         r0, r1, r2 = rows_of(rt), rows_of(rt + 1), rows_of(rt + 2)
-        inv = bc[x0, rt]
+        inv = bc[5 * nl, rt]
         pre, run = [None] * halves, [None] * halves
         ld_a, ld_b = [None] * halves, [None] * halves
         for j in range(nl):
@@ -319,10 +332,10 @@
                 after = pltpu.roll(jnp.where(bottom, tbuf[j, r2, cols], t), SUB - 1, 0)
                 before = pltpu.roll(jnp.where(top, tbuf[j, r0, cols], t), 1, 0)
                 beside = jnp.where(at_first, from_l[h], fwd[h]) + jnp.where(at_last, from_r[h], bwd[h])
-                rhs = bc[4 * nl + j, rt] * t + bc[6 * nl + j, rt]
+                rhs = bc[x0 + nl + j, rt] * t + bc[4 * nl + j, rt]
                 rhs = rhs + bc[2 * nl + j, rt] * after
-                rhs = rhs + bc[3 * nl + j, rt] * before
-                rhs = rhs + bc[5 * nl + j, rt] * beside
+                rhs = rhs + bc[x0 + j, rt] * before
+                rhs = rhs + bc[3 * nl + j, rt] * beside
                 if j == 0:
                     ld_a[h] = rhs
                 elif j == nl - 1:
@@ -344,7 +357,7 @@
         return pltpu.make_async_remote_copy(
             src_ref=src.at[k],
             dst_ref=dst.at[k],
-            send_sem=send.at[k],
+            send_sem=send,
             recv_sem=recv.at[k],
             device_id=partner,
             device_id_type=MESH,
@@ -354,84 +367,81 @@
         return pltpu.make_async_remote_copy(
             src_ref=src,
             dst_ref=dst.at[chip],
-            send_sem=send.at[k],
-            recv_sem=recv.at[chip],
+            send_sem=send,
+            recv_sem=recv,
             device_id={"stack": 2 * k + core},
             device_id_type=MESH,
         )
 
-    def from_chip(dst, send, recv, k):
+    def whole(ref, send, recv):
         return pltpu.make_async_remote_copy(
-            src_ref=dst.at[k],
-            dst_ref=dst.at[k],
-            send_sem=send.at[k],
-            recv_sem=recv.at[k],
-            device_id={"stack": 2 * k + core},
+            src_ref=ref,
+            dst_ref=ref,
+            send_sem=send,
+            recv_sem=recv,
+            device_id=partner,
             device_id_type=MESH,
         )
 
-    @pl.loop(0, nch)
-    def _(i):
-        k = lax.rem(chip + half + i, nch)
-        ld_a, ld_b = block(2 * k + other)
-        for h in range(halves):
-            cols = slice(h * LANES, (h + 1) * LANES)
-            pair_tx[k, 0, :, cols] = ld_a[h]
-            pair_tx[k, 1, :, cols] = ld_b[h]
-        to_partner(pair_tx, pair_rx, pair_send, pair_recv, k).start()
+    def inward(t):
+        return [lax.rem(chip + nch - half + t, nch), lax.rem(chip + half - 1 - t, nch)]
+
+    def outward(t):
+        return [lax.rem(chip + t, nch), lax.rem(chip + nch - 1 - t, nch)]
+
+    columns = [slice(h * LANES, (h + 1) * LANES) for h in range(halves)]
+
+    @pl.loop(0, half)
+    def _(t):
+        ks = inward(t)
+        found = [block(2 * k + other) for k in ks]
+        for k, (ld_a, ld_b) in zip(ks, found):
+            for h, cols in enumerate(columns):
+                pair_tx[k, 0, :, cols] = ld_a[h]
+                pair_tx[k, 1, :, cols] = ld_b[h]
+            to_partner(pair_tx, pair_rx, pair_send, pair_recv, k).start()
 
     if nch > 4:
         pl.semaphore_wait(ready.at[1], 2)
 
-    @pl.loop(0, nch)
-    def _(i):
-        k = lax.rem(chip + half + i, nch)
-        rows = ct.at[rows_of(2 * k + core), :]
-
-        @pl.when(k != chip)
-        def _():
-            to_chip(rows, ct_rx, ct_send, ct_recv, k).start()
-
-        @pl.when(k == chip)
-        def _():
-            ct_rx[k] = rows[...]
-
-    @pl.loop(0, nch)
-    def _(i):
-        k = lax.rem(chip + half + i, nch)
-        rt = 2 * k + core
-        ld_a, ld_b = block(rt)
-        to_partner(pair_tx, pair_rx, pair_send, pair_recv, k).wait_recv()
-        p, q, u, v = (bc[x0 + 1 + n, rt] for n in range(4))
-        for h in range(halves):
-            cols = slice(h * LANES, (h + 1) * LANES)
-            their_a, their_b = pair_rx[k, 0, :, cols], pair_rx[k, 1, :, cols]
-            f_b = jnp.where(core == 0, ld_b[h], their_b)
-            f_a = jnp.where(core == 0, their_a, ld_a[h])
-            f_lo = jnp.where(core == 0, ld_a[h], their_a)
-            f_hi = jnp.where(core == 0, their_b, ld_b[h])
-            to_lo = p * f_b + q * f_a
-            to_hi = u * f_b + v * f_a
-            inner[k, 0, :, cols] = to_lo
-            inner[k, 1, :, cols] = to_hi
-            ld_tx[k, 0, :, cols] = f_lo + to_lo
-            ld_tx[k, 1, :, cols] = f_hi + to_hi
-
-        @pl.when(k != chip)
-        def _():
-            to_chip(ld_tx.at[k], ld_rx, ld_send, ld_recv, k).start()
-
-        @pl.when(k == chip)
-        def _():
-            ld_rx[k] = ld_tx[k]
-
     @pl.loop(1, nch)
     def _(i):
-        from_chip(ct_rx, ct_send, ct_recv, lax.rem(chip + i, nch)).wait_recv()
-
+        k = lax.rem(chip + i, nch)
+        to_chip(ct.at[rows_of(2 * k + core), :], ct_rx, ct_send, ct_recv, k).start()
+
+    ct_rx[chip] = ct[rows_of(me), :]
+
+    @pl.loop(0, half)
+    def _(t):
+        ks = inward(t)
+        found = [block(2 * k + core) for k in ks]
+        for k, (ld_a, ld_b) in zip(ks, found):
+            to_partner(pair_tx, pair_rx, pair_send, pair_recv, k).wait_recv()
+            p, q, u, v = (mc[n, k] for n in range(4))
+            for h, cols in enumerate(columns):
+                their_a, their_b = pair_rx[k, 0, :, cols], pair_rx[k, 1, :, cols]
+                f_b = jnp.where(core == 0, ld_b[h], their_b)
+                f_a = jnp.where(core == 0, their_a, ld_a[h])
+                f_lo = jnp.where(core == 0, ld_a[h], their_a)
+                f_hi = jnp.where(core == 0, their_b, ld_b[h])
+                to_lo = p * f_b + q * f_a
+                to_hi = u * f_b + v * f_a
+                inner[k, 0, :, cols] = to_lo
+                inner[k, 1, :, cols] = to_hi
+                ld_tx[k, 0, :, cols] = f_lo + to_lo
+                ld_tx[k, 1, :, cols] = f_hi + to_hi
+
+            @pl.when(k != chip)
+            def _():
+                to_chip(ld_tx.at[k], ld_rx, ld_send, ld_recv, k).start()
+
+    ld_rx[chip] = ld_tx[chip]
+
+    others = pl.ds(0, nch - 1)
+    whole(ct_rx.at[others], ct_send, ct_recv).wait_recv()
     s, hold = None, None
     for d in range(nch):
-        g_lo, g_hi, gam = (lane(ct_rx[d], x0 + 7 + q) for q in range(3))
+        g_lo, g_hi, gam = (lane(ct_rx[d], len(merge) + q) for q in range(3))
         s = g_lo if d == 0 else g_lo + hold * s
         inv = 1.0 / (s + gam)
         hold = gam * inv
@@ -446,12 +456,8 @@
             hold = jnp.zeros_like(inv)
         piv[2 * d + 1, 0], piv[2 * d + 1, 1] = inv, hold
 
-    @pl.loop(1, nch)
-    def _(i):
-        from_chip(ld_rx, ld_send, ld_recv, lax.rem(chip + i, nch)).wait_recv()
-
-    for h in range(halves):
-        cols = slice(h * LANES, (h + 1) * LANES)
+    whole(ld_rx.at[others], ld_send, ld_recv).wait_recv()
+    for cols in columns:
         flow = []
         for n in range(2 * nch):
             now = ld_rx[n // 2, n % 2, :, cols]
@@ -464,22 +470,16 @@
             x = flow[n] * piv[n, 0] + piv[n, 1] * x
             sol_tx[n // 2, n % 2, :, cols] = x
 
-    @pl.loop(0, nch)
+    @pl.loop(0, nch - 1)
     def _(i):
-        k = lax.rem(chip + half + i, nch)
-
-        @pl.when(k != chip)
-        def _():
-            to_chip(sol_tx.at[k], sol_rx, sol_send, sol_recv, k).start()
-
-        @pl.when(k == chip)
-        def _():
-            sol_rx[k] = sol_tx[k]
+        k = lax.rem(chip + half + i + (i >= half), nch)
+        to_chip(sol_tx.at[k], sol_rx, sol_send, sol_recv.at[chip], k).start()
+
+    sol_rx[chip] = sol_tx[chip]
 
     def finish(rt, lo, hi):
         r = rows_of(rt)
-        for h in range(halves):
-            cols = slice(h * LANES, (h + 1) * LANES)
+        for h, cols in enumerate(columns):
             out_ref[0, r, cols] = lo[h]
             out_ref[nl - 1, r, cols] = hi[h]
             bent = hi[h] + fold[rt, :, cols]
@@ -487,50 +487,55 @@
                 ends = bc[j, rt] * lo[h] + bc[nl + j, rt] * bent
                 out_ref[j, r, cols] = out_ref[j, r, cols] + ends
 
-    @pl.loop(0, nch)
-    def _(i):
-        k = lax.rem(chip + i, nch)
-        rt = 2 * k + core
-
-        @pl.when(k != chip)
-        def _():
-            from_chip(sol_rx, sol_send, sol_recv, k).wait_recv()
-
-        p, q, u, v, s_b, s_a = (bc[x0 + 1 + n, rt] for n in range(6))
-        lo, hi = [None] * halves, [None] * halves
-        for h in range(halves):
-            cols = slice(h * LANES, (h + 1) * LANES)
-            x_lo, x_hi = sol_rx[k, 0, :, cols], sol_rx[k, 1, :, cols]
-            x_b = p * x_lo + u * x_hi + s_b * inner[k, 0, :, cols]
-            x_a = q * x_lo + v * x_hi + s_a * inner[k, 1, :, cols]
-            lo[h] = jnp.where(core == 0, x_lo, x_a)
-            hi[h] = jnp.where(core == 0, x_b, x_hi)
-            end_tx[k, 0, :, cols] = jnp.where(core == 0, x_a, x_lo)
-            end_tx[k, 1, :, cols] = jnp.where(core == 0, x_hi, x_b)
-        to_partner(end_tx, ends_buf, end_send, end_recv, k).start()
-        finish(rt, lo, hi)
-
-    @pl.loop(0, nch)
-    def _(i):
-        k = lax.rem(chip + i, nch)
-        to_partner(end_tx, ends_buf, end_send, end_recv, k).wait_recv()
-        lo = [ends_buf[k, 0, :, h * LANES : (h + 1) * LANES] for h in range(halves)]
-        hi = [ends_buf[k, 1, :, h * LANES : (h + 1) * LANES] for h in range(halves)]
-        finish(2 * k + other, lo, hi)
+    def finish_own(t):
+        ks = outward(t)
+        found = []
+        for k in ks:
+
+            @pl.when(k != chip)
+            def _():
+                to_chip(sol_tx.at[k], sol_rx, sol_send, sol_recv.at[k], k).wait_recv()
+
+            p, q, u, v, s_b, s_a = (mc[n, k] for n in range(6))
+            lo, hi = [None] * halves, [None] * halves
+            for h, cols in enumerate(columns):
+                x_lo, x_hi = sol_rx[k, 0, :, cols], sol_rx[k, 1, :, cols]
+                x_b = p * x_lo + u * x_hi + s_b * inner[k, 0, :, cols]
+                x_a = q * x_lo + v * x_hi + s_a * inner[k, 1, :, cols]
+                lo[h] = jnp.where(core == 0, x_lo, x_a)
+                hi[h] = jnp.where(core == 0, x_b, x_hi)
+                end_tx[k, 0, :, cols] = jnp.where(core == 0, x_a, x_lo)
+                end_tx[k, 1, :, cols] = jnp.where(core == 0, x_hi, x_b)
+            to_partner(end_tx, ends_buf, end_send, end_recv, k).start()
+            found.append((lo, hi))
+        for k, (lo, hi) in zip(ks, found):
+            finish(2 * k + core, lo, hi)
+
+    def finish_theirs(t):
+        ks = outward(t)
+        for k in ks:
+            to_partner(end_tx, ends_buf, end_send, end_recv, k).wait_recv()
+        for k in ks:
+            lo = [ends_buf[k, 0, :, cols] for cols in columns]
+            hi = [ends_buf[k, 1, :, cols] for cols in columns]
+            finish(2 * k + other, lo, hi)
+
+    finish_own(0)
+
+    @pl.loop(1, half)
+    def _(t):
+        finish_own(t)
+        finish_theirs(t - 1)
+
+    finish_theirs(half - 1)
 
     for copy in (comp, row_dn, row_up, cor_dn, cor_up, edge_r, edge_l):
         copy.wait_send()
-
-    @pl.loop(0, nch)
-    def _(k):
-        to_partner(pair_tx, pair_rx, pair_send, pair_recv, k).wait_send()
-        to_partner(end_tx, ends_buf, end_send, end_recv, k).wait_send()
-
-        @pl.when(k != chip)
-        def _():
-            to_chip(ct.at[rows_of(2 * k + core), :], ct_rx, ct_send, ct_recv, k).wait_send()
-            to_chip(ld_tx.at[k], ld_rx, ld_send, ld_recv, k).wait_send()
-            to_chip(sol_tx.at[k], sol_rx, sol_send, sol_recv, k).wait_send()
+    whole(pair_tx, pair_send, ct_recv).wait_send()
+    whole(end_tx, end_send, ct_recv).wait_send()
+    whole(ct_rx.at[others], ct_send, ct_recv).wait_send()
+    whole(ld_tx.at[others], ld_send, ct_recv).wait_send()
+    whole(sol_tx.at[others], sol_send, ct_recv).wait_send()
 
 
 def copy_out(parts, x_ref, out_ref, sem):
@@ -581,17 +586,27 @@
             pltpu.VMEM((LANES, nr), f32),
             pltpu.VMEM((nr, LANES), f32),
             pltpu.VMEM((nch, SUB, LANES), f32),
-            pltpu.VMEM((7 * nl + 7, tiles, SUB, LANES), f32),
+            pltpu.VMEM((7 * nl + 1, tiles, SUB, LANES), f32),
+            pltpu.VMEM((6, nch, SUB, LANES), f32),
             pltpu.VMEM((tiles, SUB, nc), f32),
         ]
         + [tile_pair] * 9
         + [
             pltpu.VMEM((2 * nch, 2, SUB, LANES), f32),
-            dma,
+            dma((LOADS,)),
             dma((7,)),
             dma((7,)),
+            dma,
+            dma,
+            dma,
+            dma((nch,)),
+            dma,
+            dma,
+            dma,
+            dma((nch,)),
+            dma,
+            dma((nch,)),
         ]
-        + [dma((nch,))] * 10
         + [pltpu.SemaphoreType.REGULAR((2,))],
         compiler_params=pltpu.CompilerParams(
             collective_id=0,

time: 52.3 us -> 35.9 us (0.69)
  Pallas kernels: 52.1 us -> 35.8 us
    pallas_call x1, Pallas kernels: 50.7 us -> 34.4 us  [per_device(): pl.pallas_call(functools.partial(kernel, dims), out_shape=pltpu.VMEM((nl,...]
where the time goes in v3:
time: 35.9 us; the launch traced here: 35.8 us
  Pallas kernels  35.8 us (100%)
    pallas_call x1, Pallas kernels, per_device(): pl.pallas_call(functools.partial(kernel, dims), out_shape=pltpu.VMEM((nl,...  34.4 us
    pallas_call x1, Pallas kernels, per_device(): pl.pallas_call(functools.partial(copy_out, parts), out_shape=jax.ShapeDty...  1.35 us

profile of v3, /device:TPU:1, one launch (start us, length us, event | category | flops | bytes accessed | tf_op | source)
XLA Modules:
  0.0 35.8 jit_solution(8611906453598262112)
XLA Ops:
  0.0 34.4 %stack_step.1.x_ref = f32[16,128,256]{2,1,0:T(8,128)S(1)} custom-call(s32[256]{0:T(256)} %cat_ref.1, s32[16,128]{1,0:T(8,128)} %corr_ref.1, f32[16,128,256]{2,1,0:T(8,128)} %t_hbm.1), custom_call_target="tpu_custom_call" | custom-call | tf_op jit(solution)/shard_map/stack_step/pallas_call | solution.py:566
  34.4 1.3 %copy_out.1 = f32[16,128,256]{2,1,0:T(8,128)} custom-call(f32[16,128,256]{2,1,0:T(8,128)S(1)} %stack_step.1.x_ref), custom_call_target="tpu_custom_call" | custom-call | tf_op jit(solution)/shard_map/copy_out/pallas_call | solution.py:619
